TPU v7x, 128 devices: a whole 4x4x4 slice. The times are simulated.
128 devices in a mesh: il: 8 (over x, core), xl: 16 (over z, y).
Axes of the slice: x: 4, y: 4, z: 4, core: 2. Of those that a mesh axis runs over, the one named last changes fastest.
Arguments:
- traces: bfloat16 [983040, 128], P(('il', 'xl')), may hold values from -6 to 6
- filter_taps: float32 [12, 64], replicated, may hold values from -1.5 to 1.5
- slot_block: int32 [128, 128, 2], P(('il', 'xl')), may hold values from 0 to 59
- slot_cells: int32 [128, 128, 2, 128], P(('il', 'xl')), may hold values from -1 to 1535
- pair_count: int32 [128, 128], P(('il', 'xl')), may hold values from 0 to 2, as said below
Outputs:
- structure_tensor: float32 [6, 256, 768, 128], P(None, 'il', 'xl')
- adjoint_traces: float32 [983040, 128], P(('il', 'xl'))
Inputs may be any that keep to these rules, and one draw needn't show every extreme that they name: Slots 0 to pair_count[e, d] - 1 of device e toward tile d are live; at most 2, and for some tiles every device sends 2 live slots.
All inputs are finite; a program needn't handle non-finite values.
Results may differ from a plain program's by a relative error of at most 0.0004.
The roundings to bfloat16 on the way count: a program that leaves them out, or rounds other values in their place, can miss the bound.
Values may be sent and summed in bfloat16 or wider, within the bound.
A program may use at most 128 MiB of HBM per device.

v0:
```python
import jax
import jax.numpy as jnp
from jax import lax
from jax.sharding import PartitionSpec as P

CIL = 32
CXL = 48


def with_halo(block, sides, width):
    for axis, dim in sides:
        count = lax.axis_size(axis)
        forward = [(i, i + 1) for i in range(count - 1)]
        backward = [(target, source) for source, target in forward]
        low = lax.ppermute(
            lax.slice_in_dim(block, block.shape[dim] - width, None, axis=dim), axis, forward
        )
        high = lax.ppermute(lax.slice_in_dim(block, 0, width, axis=dim), axis, backward)
        block = jnp.concatenate([low, block, high], axis=dim)
    return block


def filter_matrices(filter_taps, samples):
    lag_table = (
        jnp.arange(samples, dtype=jnp.int32)[None, :]
        - jnp.arange(samples, dtype=jnp.int32)[:, None]
    )
    tap_count = filter_taps.shape[1]
    inside = (lag_table >= 0) & (lag_table < tap_count)
    picked = filter_taps[:, jnp.clip(lag_table, 0, tap_count - 1)]
    return jnp.where(inside[None], picked, 0.0).astype(jnp.bfloat16)


def cycle_box(values, rows_out, cols_out):
    box_total = jnp.zeros((rows_out, cols_out, values.shape[2]), jnp.float32)
    for row_shift in range(3):
        for col_shift in range(3):
            box_total = (
                box_total
                + values[row_shift : row_shift + rows_out, col_shift : col_shift + cols_out]
            )
    return box_total / 9.0


def local(traces, filter_taps, slot_block, slot_cells, pair_count):
    count_il = lax.axis_size("il")
    count_xl = lax.axis_size("xl")
    devices = count_il * count_xl
    samples = traces.shape[1]
    row_block = slot_cells.shape[3]
    capacity = slot_block.shape[2]
    surveys = filter_taps.shape[0]
    blocks_here = traces.shape[0] // row_block
    cell_count = CIL * CXL
    group_size = 16
    slot_total = devices * capacity
    group_count = slot_total // group_size
    matrices = filter_matrices(filter_taps, samples)
    by_survey = traces.reshape(surveys, blocks_here // surveys * row_block, samples)
    filtered = jnp.einsum("sru,sut->srt", by_survey, matrices, preferred_element_type=jnp.float32)
    filtered = filtered.astype(jnp.bfloat16).reshape(blocks_here, row_block, samples)
    block_ids = slot_block[0].reshape(-1)
    outgoing = jnp.take(filtered, block_ids, axis=0).reshape(devices, capacity, row_block, samples)
    slot_live = jnp.arange(capacity, dtype=jnp.int32)[None, :] < pair_count[0][:, None]
    out_cells = jnp.where(slot_live[:, :, None], slot_cells[0], -1)
    incoming, in_cells = (
        lax.all_to_all(outgoing, ("il", "xl"), split_axis=0, concat_axis=0, tiled=True),
        lax.all_to_all(out_cells, ("il", "xl"), split_axis=0, concat_axis=0, tiled=True),
    )
    incoming = incoming.reshape(slot_total, row_block, samples)
    in_cells = in_cells.reshape(slot_total, row_block)
    cell_line = jnp.arange(cell_count, dtype=jnp.int32)

    def one_hot(group_cells):
        return (cell_line[:, None] == group_cells.reshape(1, -1)).astype(jnp.bfloat16)

    def add_group(running, group_blocks, group_cells):
        stacked, fold_counts = running
        selector = one_hot(group_cells)
        stacked = stacked + jnp.dot(
            selector, group_blocks.reshape(-1, samples), preferred_element_type=jnp.float32
        )
        fold_counts = fold_counts + jnp.sum(selector, axis=1, dtype=jnp.float32)
        return (stacked, fold_counts)

    initial = (jnp.zeros((cell_count, samples), jnp.float32), jnp.zeros((cell_count,), jnp.float32))

    def scan_step(running, scan_item):
        return (add_group(running, scan_item[0], scan_item[1]), None)

    (stacked, fold_counts), unused = lax.scan(
        scan_step,
        initial,
        (
            incoming.reshape(group_count, group_size, row_block, samples),
            in_cells.reshape(group_count, group_size, row_block),
        ),
    )
    stack_image = stacked / jnp.maximum(fold_counts, 1.0)[:, None]
    image_half = stack_image.astype(jnp.bfloat16)

    def read_group(group_cells):
        selector = one_hot(group_cells)
        picked = lax.dot_general(
            selector, image_half, (((0,), (0,)), ((), ())), preferred_element_type=jnp.float32
        )
        return picked.astype(jnp.bfloat16).reshape(group_size, row_block, samples)

    answer = lax.map(read_group, in_cells.reshape(group_count, group_size, row_block)).reshape(
        slot_total, row_block, samples
    )
    returned = lax.all_to_all(
        answer.reshape(devices, capacity, row_block, samples),
        ("il", "xl"),
        split_axis=0,
        concat_axis=0,
        tiled=True,
    )
    returned = returned.reshape(slot_total, row_block, samples)
    out_valid = (out_cells >= 0).reshape(slot_total, row_block, 1)
    zero_half = jnp.zeros((), jnp.bfloat16)
    sent_part = jnp.where(out_valid, outgoing.reshape(slot_total, row_block, samples), zero_half)
    back_part = jnp.where(out_valid, returned, zero_half)
    selector_rows = (
        block_ids[:, None] == jnp.arange(blocks_here, dtype=jnp.int32)[None, :]
    ).astype(jnp.bfloat16)
    residual = jnp.einsum(
        "sb,sit->bit", selector_rows, sent_part, preferred_element_type=jnp.float32
    )
    residual = residual - jnp.einsum(
        "sb,sit->bit", selector_rows, back_part, preferred_element_type=jnp.float32
    )
    residual_half = residual.astype(jnp.bfloat16).reshape(surveys, -1, samples)
    adjoint_traces = jnp.einsum(
        "srt,sut->sru", residual_half, matrices, preferred_element_type=jnp.float32
    ).reshape(traces.shape)
    tile_image = stack_image.reshape(CIL, CXL, samples)
    padded = with_halo(tile_image, (("il", 0), ("xl", 1)), 2)
    padded_time = jnp.pad(padded, ((0, 0), (0, 0), (1, 1)))
    grad_il = (padded[2:, 1:-1] - padded[:-2, 1:-1]) * 0.5
    grad_xl = (padded[1:-1, 2:] - padded[1:-1, :-2]) * 0.5
    grad_time = (padded_time[1:-1, 1:-1, 2:] - padded_time[1:-1, 1:-1, :-2]) * 0.5
    rows_il = lax.axis_index("il") * CIL + jnp.arange(CIL + 2, dtype=jnp.int32) - 1
    rows_xl = lax.axis_index("xl") * CXL + jnp.arange(CXL + 2, dtype=jnp.int32) - 1
    inside_il = ((rows_il >= 0) & (rows_il < CIL * count_il)).astype(jnp.float32)
    inside_xl = ((rows_xl >= 0) & (rows_xl < CXL * count_xl)).astype(jnp.float32)
    cycle_mask = inside_il[:, None, None] * inside_xl[None, :, None]
    factor_pairs = (
        (grad_il, grad_il),
        (grad_xl, grad_xl),
        (grad_time, grad_time),
        (grad_il, grad_xl),
        (grad_il, grad_time),
        (grad_xl, grad_time),
    )
    structure_tensor = jnp.stack(
        [
            cycle_box(left_part * right_part * cycle_mask, CIL, CXL)
            for left_part, right_part in factor_pairs
        ]
    )
    return (structure_tensor, adjoint_traces)


def solution(mesh):
    return jax.shard_map(
        local,
        mesh=mesh,
        in_specs=(
            P(("il", "xl"), None),
            P(),
            P(("il", "xl"), None, None),
            P(("il", "xl"), None, None, None),
            P(("il", "xl"), None),
        ),
        out_specs=(P(None, "il", "xl", None), P(("il", "xl"), None)),
        check_vma=False,
    )
```

profile of v0, /device:TPU:62, one launch (start us, length us, event | category | flops | bytes accessed | tf_op | source)
XLA Modules:
  0.0 526.8 jit_solution(12338355533591361531)
XLA Ops:
  3.3 10.0 %all-to-all-start = ((s32[128,2,128]{2,1,0:T(2,128)}), s32[128,2,128]{2,1,0:T(2,128)S(1)}, u32[]{:S(2)}, u32[]{:S(2)}) async-start(s32[128,2,128]{2,1,0:T(2,128)} %bitcast_select_fusion.1), calls=%async_computation | async-start | bytes 262144 | tf_op jit(solution)/shard_map/all_to_all | solution.py:68
  16.0 57.9 %gather_fusion = bf16[16384,12]{1,0:T(8,128)(2,1)} fusion(bf16[12,64]{0,1:T(8,128)(2,1)S(1)} %copy.25, s32[16384]{0:T(1024)S(1)} %fusion.45), kind=kCustom, calls=%fused_computation | custom fusion | bytes 851968 | tf_op jit(solution)/shard_map/gather | solution.py:30
  73.9 3.8 copy.26
  79.8 2.8 copy.28
  82.6 8.6 %gather_fusion.1 = bf16[256,128,128]{2,1,0:T(8,128)(2,1)} fusion(bf16[60,128,128]{2,1,0:T(8,128)(2,1)S(1)} %bitcast.83, s32[1024]{0:T(1024)S(1)} %pad_clamp_fusion), kind=kCustom, calls=%fused_computation.1 | custom fusion | bytes 16778240 | tf_op jit(solution)/shard_map/jit(_take)/gather | solution.py:63
  91.3 7.4 %broadcast_select_fusion = bf16[128,2,128,128]{3,2,1,0:T(8,128)(2,1)} fusion(bf16[128,2,128,128]{3,2,1,0:T(8,128)(2,1)} %bitcast.82, pred[128,2]{1,0:T(8,128)(4,1)S(1)} %copy.24), kind=kLoop, calls=%fused_computation.25 | loop fusion | flops 4194304 | bytes 16777472 | tf_op jit(solution)/shard_map/jit(_take)/select_n | solution.py:63
  98.7 10.9 %all-to-all-start.1 = ((bf16[128,2,128,128]{3,2,1,0:T(8,128)(2,1)}), bf16[128,2,128,128]{3,2,1,0:T(8,128)(2,1)}, u32[]{:S(2)}, u32[]{:S(2)}) async-start(bf16[128,2,128,128]{3,2,1,0:T(8,128)(2,1)} %broadcast_select_fusion), calls=%async_computation.1 | async-start | bytes 16777216 | tf_op jit(solution)/shard_map/all_to_all | solution.py:67
  109.6 99.5 %all-to-all-done.1 = bf16[128,2,128,128]{3,2,1,0:T(8,128)(2,1)} async-done(((bf16[128,2,128,128]{3,2,1,0:T(8,128)(2,1)}), bf16[128,2,128,128]{3,2,1,0:T(8,128)(2,1)}, u32[]{:S(2)}, u32[]{:S(2)}) %all-to-all-start.1) | async-done | bytes 8388640 | tf_op jit(solution)/shard_map/all_to_all | solution.py:67
  209.1 79.6 %while.25 = (s32[]{:T(128)}, f32[1536,128]{1,0:T(8,128)S(1)}, f32[1536]{0:T(1024)S(1)}, s32[16,16,128]{2,1,0:T(8,128)S(1)}, bf16[16,16,128,128]{3,2,1,0:T(8,128)(2,1)}, /*index=5*/s32[]{:T(128)}, s32[]{:T(128)}) while((s32[]{:T(128)}, f32[1536,128]{1,0:T(8,128)S(1)}, f32[1536]{0:T(1024)S(1)}, s32[16,16,128]{2,1,0:T(8,128)S(1)}, ...), condition=%wide.region_2.3_spmd.clone, body=%wide.region_0.2_spmd.clone.sunk | while | flops 821429760 | bytes 3203176 | solution.py:91
  211.5 2.5 fusion.69
  216.5 2.5 fusion.69
  221.5 2.5 fusion.69
  226.5 2.5 fusion.69
  231.5 2.5 fusion.69
  236.4 2.5 fusion.69
  241.4 2.5 fusion.69
  246.4 2.5 fusion.69
  251.4 2.5 fusion.69
  261.3 2.5 fusion.69
  266.3 2.5 fusion.69
  271.3 2.5 fusion.69
  276.3 2.5 fusion.69
  289.0 69.1 %while.24 = (s32[]{:T(128)}, bf16[16,16,128,128]{3,2,1,0:T(8,128)(2,1)}, s32[16,16,128]{2,1,0:T(8,128)S(1)}, bf16[1536,128]{1,0:T(8,128)(2,1)S(1)}, s32[]{:T(128)}) while((s32[]{:T(128)}, bf16[16,16,128,128]{3,2,1,0:T(8,128)(2,1)}, s32[16,16,128]{2,1,0:T(8,128)S(1)}, bf16[1536,128]{1,0:T(8,128)(2,1)S(1)}, s32[]{:T(128)}) %tuple.57), condition=%wide.region_4.5_spmd.clone, body=%wide.region_3.4_spmd.clone.sunk | while | flops 808714240 | bytes 1990733 | solution.py:109
  289.1 3.4 fusion.67
  293.4 3.4 fusion.67
  297.7 3.4 fusion.67
  302.0 3.4 fusion.67
  306.3 3.4 fusion.67
  310.6 3.4 fusion.67
  314.9 3.4 fusion.67
  319.2 3.4 fusion.67
  323.5 3.4 fusion.67
  327.9 3.4 fusion.67
  332.2 3.4 fusion.67
  336.5 3.4 fusion.67
  340.8 3.4 fusion.67
  345.1 3.4 fusion.67
  349.5 3.4 fusion.67
  353.8 3.4 fusion.67
  358.1 12.6 %all-to-all-start.2 = ((bf16[128,2,128,128]{3,2,1,0:T(8,128)(2,1)}), bf16[128,2,128,128]{3,2,1,0:T(8,128)(2,1)}, u32[]{:S(2)}, u32[]{:S(2)}) async-start(bf16[128,2,128,128]{3,2,1,0:T(8,128)(2,1)} %bitcast.90), calls=%async_computation.2 | async-start | bytes 16777216 | tf_op jit(solution)/shard_map/all_to_all | solution.py:112
  375.7 90.9 %collective-permute-done.1 = f32[2,48,128]{2,1,0:T(8,128)S(1)} collective-permute-done((f32[2,48,128]{2,1,0:T(8,128)S(1)}, f32[2,48,128]{2,1,0:T(8,128)S(1)}, u32[]{:S(2)}, u32[]{:S(2)}) %collective-permute-start.1) | collective-permute-done | bytes 49184 | tf_op jit(solution)/shard_map/ppermute | solution.py:18
  466.6 3.7 collective-permute-done
  470.3 3.8 collective-permute-start.2
  476.4 5.7 %collective-permute-done.3 = f32[36,2,128]{2,1,0:T(2,128)S(1)} collective-permute-done((f32[36,2,128]{2,1,0:T(2,128)S(1)}, f32[36,2,128]{2,1,0:T(2,128)S(1)}, u32[]{:S(2)}, u32[]{:S(2)}) %collective-permute-start.3) | collective-permute-done | bytes 36896 | tf_op jit(solution)/shard_map/ppermute | solution.py:18
  492.1 7.3 %select_select_fusion = (bf16[256,128,128]{2,1,0:T(8,128)(2,1)S(1)}, bf16[256,128,128]{2,1,0:T(8,128)(2,1)S(1)}) fusion(bf16[256,128,128]{2,1,0:T(8,128)(2,1)} %gather_fusion.1, pred[256]{0:T(512)(128)(4,1)S(1)} %compare_and_fusion, pred[256,128]{1,0:T(8,128)(4,1)S(1)} %select_compare_fusion, bf16[128,2,128,128]{3,2,1,0:T(8,128)(2,1)} %all-to-all-done.2), kind=kLoop, calls=%fused_computation.24 | loop fusion | flops 12582912 | bytes 33587456 | tf_op jit(solution)/shard_map/jit(_where)/select_n | solution.py:122
  499.4 5.0 fusion.11
  504.4 18.3 %subtract_convert_fusion = bf16[60,128,128]{2,0,1:T(8,128)(2,1)S(1)} fusion(f32[60,128,128]{2,0,1:T(8,128)S(1)} %fusion.11, bf16[256,128,128]{2,1,0:T(8,128)(2,1)S(1)} %get-tuple-element.125, s32[256]{0:T(256)S(1)} %reshape_squeeze.9), kind=kOutput, calls=%fused_computation.26 | convolution fusion | flops 505297920 | bytes 14287872 | tf_op jit(solution)/shard_map/sb,sit->bit/dot_general | solution.py:127
  524.0 2.6 fusion.41
  (147 shorter events, 86.3 us)
Async XLA Ops:
  0.6 77.0 %copy-start = (bf16[7680,128]{1,0:T(8,128)(2,1)S(1)}, bf16[7680,128]{1,0:T(8,128)(2,1)}, u32[]{:S(2)}) copy-start(bf16[7680,128]{1,0:T(8,128)(2,1)} %param.9) | copy-start | bytes 5898244
  3.3 95.4 %all-to-all-start = ((s32[128,2,128]{2,1,0:T(2,128)}), s32[128,2,128]{2,1,0:T(2,128)S(1)}, u32[]{:S(2)}, u32[]{:S(2)}) async-start(s32[128,2,128]{2,1,0:T(2,128)} %bitcast_select_fusion.1), calls=%async_computation | async-start | bytes 262144 | tf_op jit(solution)/shard_map/all_to_all | solution.py:68
  98.7 110.4 %all-to-all-start.1 = ((bf16[128,2,128,128]{3,2,1,0:T(8,128)(2,1)}), bf16[128,2,128,128]{3,2,1,0:T(8,128)(2,1)}, u32[]{:S(2)}, u32[]{:S(2)}) async-start(bf16[128,2,128,128]{3,2,1,0:T(8,128)(2,1)} %broadcast_select_fusion), calls=%async_computation.1 | async-start | bytes 16777216 | tf_op jit(solution)/shard_map/all_to_all | solution.py:67
  358.1 12.8 %copy-start.2 = (s32[1,128,2,128]{3,2,1,0:T(2,128)S(1)}, s32[1,128,2,128]{3,2,1,0:T(2,128)}, u32[]{:S(2)}) copy-start(s32[1,128,2,128]{3,2,1,0:T(2,128)} %param.12) | copy-start | bytes 393220
  358.1 134.0 %all-to-all-start.2 = ((bf16[128,2,128,128]{3,2,1,0:T(8,128)(2,1)}), bf16[128,2,128,128]{3,2,1,0:T(8,128)(2,1)}, u32[]{:S(2)}, u32[]{:S(2)}) async-start(bf16[128,2,128,128]{3,2,1,0:T(8,128)(2,1)} %bitcast.90), calls=%async_computation.2 | async-start | bytes 16777216 | tf_op jit(solution)/shard_map/all_to_all | solution.py:112
  371.0 95.5 %collective-permute-start.1 = (f32[2,48,128]{2,1,0:T(8,128)S(1)}, f32[2,48,128]{2,1,0:T(8,128)S(1)}, u32[]{:S(2)}, u32[]{:S(2)}) collective-permute-start(f32[2,48,128]{2,1,0:T(8,128)S(1)} %bitcast.97), channel_id=1, source_target_pairs={{16,0},{32,16},{48,32},{64,48},{80,64},{96,80},{112,96},{17,1},{33... | collective-permute-start | bytes 147464 | tf_op jit(solution)/shard_map/ppermute | solution.py:18
  373.5 96.8 %collective-permute-start = (f32[2,48,128]{2,1,0:T(8,128)S(1)}, f32[2,48,128]{2,1,0:T(8,128)S(1)}, u32[]{:S(2)}, u32[]{:S(2)}) collective-permute-start(f32[2,48,128]{2,1,0:T(8,128)S(1)} %bitcast.96), channel_id=1, source_target_pairs={{0,16},{16,32},{32,48},{48,64},{64,80},{80,96},{96,112},{1,17},{17... | collective-permute-start | bytes 147464 | tf_op jit(solution)/shard_map/ppermute | solution.py:15
  470.3 6.0 %collective-permute-start.2 = (f32[36,2,128]{2,1,0:T(2,128)S(1)}, f32[36,2,128]{2,1,0:T(2,128)S(1)}, u32[]{:S(2)}, u32[]{:S(2)}) collective-permute-start(f32[36,2,128]{2,1,0:T(2,128)S(1)} %get-tuple-element.121), channel_id=1, source_target_pairs={{0,1},{1,2},{2,3},{3,4},{4,5},{5,6},{6,7},{7,8},{8,9},{9,10},{10,1... | collective-permute-start | bytes 110600 | tf_op jit(solution)/shard_map/ppermute | solution.py:15
  474.1 8.0 %collective-permute-start.3 = (f32[36,2,128]{2,1,0:T(2,128)S(1)}, f32[36,2,128]{2,1,0:T(2,128)S(1)}, u32[]{:S(2)}, u32[]{:S(2)}) collective-permute-start(f32[36,2,128]{2,1,0:T(2,128)S(1)} %get-tuple-element.122), channel_id=1, source_target_pairs={{1,0},{2,1},{3,2},{4,3},{5,4},{6,5},{7,6},{8,7},{9,8},{10,9},{11,1... | collective-permute-start | bytes 110600 | tf_op jit(solution)/shard_map/ppermute | solution.py:18
  504.4 22.2 %copy-start.1 = (bf16[7680,128]{1,0:T(8,128)(2,1)S(1)}, bf16[7680,128]{1,0:T(8,128)(2,1)}, u32[]{:S(2)}) copy-start(bf16[7680,128]{1,0:T(8,128)(2,1)} %param.9) | copy-start | bytes 5898244
where the time goes:
time: 533 us; the launch traced here: 527 us
  waiting for transfers between devices  200 us (38%)
  matrix products  123 us (23%)
  local copies, waits for them, and re-layouts  108 us (20%)
  other arithmetic  49.9 us (9%)
  starting transfers between devices  43.9 us (8%)
    all_to_all x1, waiting for transfers between devices, local(): lax.all_to_all(outgoing, ('il', 'xl'), split_axis=0, concat_axis=0, tiled...  99.5 us
    ppermute x2, waiting for transfers between devices, with_halo(): lax.ppermute(lax.slice_in_dim(block, 0, width, axis=dim), axis, backward)  96.6 us
    gather x2, local copies, waits for them, and re-layouts, filter_matrices(): picked = filter_taps[:, jnp.clip(lag_table, 0, tap_count - 1)]  61.7 us
    dot_general x16, matrix products, read_group(): lax.dot_general(selector, image_half, (((0,), (0,)), ((), ())), preferred...  55.1 us
    dot_general x16, matrix products, add_group(): jnp.dot(selector, group_blocks.reshape(-1, samples), preferred_element_ty...  40.1 us
    reduce_sum x16, other arithmetic, add_group(): fold_counts = fold_counts + jnp.sum(selector, axis=1, dtype=jnp.float32)  21.1 us
    dot_general x1, matrix products, local(): jnp.einsum('sb,sit->bit', selector_rows, sent_part, preferred_element_typ...  18.3 us
    dynamic_slice x16, local copies, waits for them, and re-layouts, local(): lax.scan(scan_step, initial, (incoming.reshape(group_count, group_size, r...  17.4 us
  transfers between devices with their start and end apart: 7, of which 4 were waited for; matrix products, arithmetic and copies ran while one was open for 18% of the time, Pallas kernels for 0%

commit v1 on v0

v1 whole, which is shorter than its diff:
```python
import functools

import jax
import jax.numpy as jnp
from jax import lax
from jax.experimental import pallas as pl
from jax.experimental.pallas import tpu as pltpu
from jax.sharding import PartitionSpec as P

CIL = 32
CXL = 48
LOW = 256
GROUP = 8
BF = jnp.bfloat16
F32 = jnp.float32


def prep_kernel(blocks, traces, rev, out0, out1, filt, mats):
    surveys = mats.shape[0]
    samples = mats.shape[1]
    rows = traces.shape[0] // surveys
    per = rows // samples
    tiles = out0.shape[0]
    step = pl.program_id(0)

    @pl.when(step == 0)
    def _():
        t_id = lax.broadcasted_iota(jnp.int32, (samples, samples), 0)
        u_id = lax.broadcasted_iota(jnp.int32, (samples, samples), 1)
        for s in range(surveys):
            base = jnp.broadcast_to(rev[s : s + 1, :], (samples, samples))
            skew = pltpu.roll(base, 0, 1, stride=1, stride_axis=0)
            mat = jnp.where(u_id <= t_id, skew, 0.0).astype(BF)
            mats[s] = mat
            res = lax.dot_general(
                mat,
                traces[s * rows : (s + 1) * rows, :],
                (((1,), (1,)), ((), ())),
                preferred_element_type=F32,
            ).astype(BF)
            for b in range(per):
                filt[s * per + b] = res[:, b * samples : (b + 1) * samples]

    for k in range(tiles):
        d = step * tiles + k
        out0[k] = filt[blocks[2 * d]]
        out1[k] = filt[blocks[2 * d + 1]]


def prep(traces, rev, blocks, surveys, samples, devices):
    tiles = 8
    nblk = traces.shape[0] // samples
    full = lambda *shape: pl.BlockSpec(shape, lambda i, *_: (0,) * len(shape))
    out = pl.BlockSpec((tiles, samples, samples), lambda i, *_: (i, 0, 0))
    return pl.pallas_call(
        prep_kernel,
        grid_spec=pltpu.PrefetchScalarGridSpec(
            num_scalar_prefetch=1,
            grid=(devices // tiles,),
            in_specs=[full(*traces.shape), full(*rev.shape)],
            out_specs=[
                out,
                out,
                full(nblk, samples, samples),
                full(surveys, samples, samples),
            ],
        ),
        out_shape=[
            jax.ShapeDtypeStruct((devices, samples, samples), BF),
            jax.ShapeDtypeStruct((devices, samples, samples), BF),
            jax.ShapeDtypeStruct((nblk, samples, samples), BF),
            jax.ShapeDtypeStruct((surveys, samples, samples), BF),
        ],
        name="prep",
    )(blocks, traces, rev)


def low_hot(cells, lanes):
    ids = lax.broadcasted_iota(jnp.int32, (LOW, lanes), 0)
    return (ids == (cells & (LOW - 1))).astype(F32).astype(BF)


def fill(cells, data, left, hot):
    group, samples, lanes = data.shape
    highs = (left.shape[0] - 16) // samples
    ids = lax.broadcasted_iota(jnp.int32, (16, lanes), 0)
    for g in range(group):
        at = slice(g * lanes, (g + 1) * lanes)
        here = cells[g : g + 1, :]
        high = here >> 8
        hot[:, at] = low_hot(here, lanes)
        block = data[g]
        masks = (ids == high).astype(F32).astype(BF)
        left[highs * samples :, at] = masks
        for h in range(highs):
            left[h * samples : (h + 1) * samples, at] = block * jnp.broadcast_to(
                (high == h).astype(F32).astype(BF), block.shape
            )


def bin_first_kernel(cells, data, acc, left, hot):
    @pl.when(pl.program_id(0) == 0)
    def _():
        acc[...] = jnp.zeros_like(acc)

    fill(cells, data, left, hot)
    acc[...] += lax.dot_general(
        left[...], hot[...], (((1,), (1,)), ((), ())), preferred_element_type=F32
    )


def bin_last_kernel(cells, data, before, half, image, acc, left, hot):
    @pl.when(pl.program_id(0) == 0)
    def _():
        acc[...] = before[...]

    fill(cells, data, left, hot)
    acc[...] += lax.dot_general(
        left[...], hot[...], (((1,), (1,)), ((), ())), preferred_element_type=F32
    )

    @pl.when(pl.program_id(0) == pl.num_programs(0) - 1)
    def _():
        samples = data.shape[1]
        highs = half.shape[0] // samples
        for h in range(highs):
            fold = acc[highs * samples + h : highs * samples + h + 1, :]
            value = acc[h * samples : (h + 1) * samples, :] / jnp.maximum(fold, 1.0)
            half[h * samples : (h + 1) * samples, :] = value.astype(BF)
            image[h * LOW : (h + 1) * LOW, :] = value.T


def bin_specs(data):
    slots, samples, lanes = data.shape
    cells_spec = pl.BlockSpec((GROUP, lanes), lambda i: (i, 0))
    data_spec = pl.BlockSpec((GROUP, samples, lanes), lambda i: (i, 0, 0))
    return cells_spec, data_spec, slots // GROUP


def bin_first(cells, data, cell_count):
    cells_spec, data_spec, steps = bin_specs(data)
    samples, lanes = data.shape[1:]
    tall = cell_count // LOW * samples + 16
    return pl.pallas_call(
        bin_first_kernel,
        grid=(steps,),
        in_specs=[cells_spec, data_spec],
        out_specs=pl.BlockSpec((tall, LOW), lambda i: (0, 0)),
        out_shape=jax.ShapeDtypeStruct((tall, LOW), F32),
        scratch_shapes=[
            pltpu.VMEM((tall, GROUP * lanes), BF),
            pltpu.VMEM((LOW, GROUP * lanes), BF),
        ],
        cost_estimate=pl.CostEstimate(
            flops=2 * data.shape[0] * lanes * tall * LOW,
            bytes_accessed=data.size * 2,
            transcendentals=0,
        ),
        name="bin_first",
    )(cells, data)


def bin_last(cells, data, before, cell_count):
    cells_spec, data_spec, steps = bin_specs(data)
    samples, lanes = data.shape[1:]
    tall = cell_count // LOW * samples + 16
    return pl.pallas_call(
        bin_last_kernel,
        grid=(steps,),
        in_specs=[cells_spec, data_spec, pl.BlockSpec((tall, LOW), lambda i: (0, 0))],
        out_specs=[
            pl.BlockSpec((tall - 16, LOW), lambda i: (0, 0)),
            pl.BlockSpec((cell_count, samples), lambda i: (0, 0)),
        ],
        out_shape=[
            jax.ShapeDtypeStruct((tall - 16, LOW), BF),
            jax.ShapeDtypeStruct((cell_count, samples), F32),
        ],
        scratch_shapes=[
            pltpu.VMEM((tall, LOW), F32),
            pltpu.VMEM((tall, GROUP * lanes), BF),
            pltpu.VMEM((LOW, GROUP * lanes), BF),
        ],
        cost_estimate=pl.CostEstimate(
            flops=2 * data.shape[0] * lanes * tall * LOW,
            bytes_accessed=data.size * 2,
            transcendentals=0,
        ),
        name="bin_last",
    )(cells, data, before)


def read_kernel(cells, half, out, hot):
    group, samples, lanes = out.shape
    highs = half.shape[0] // samples
    for g in range(group):
        hot[:, g * lanes : (g + 1) * lanes] = low_hot(cells[g : g + 1, :], lanes)
    for g in range(group):
        wide = jnp.dot(
            half[...], hot[:, g * lanes : (g + 1) * lanes], preferred_element_type=F32
        )
        high = jnp.broadcast_to(cells[g : g + 1, :] >> 8, (samples, lanes))
        picked = jnp.zeros((samples, lanes), F32)
        for h in range(highs):
            picked = jnp.where(high == h, wide[h * samples : (h + 1) * samples, :], picked)
        out[g] = picked.astype(BF)


def read(cells, half, samples):
    slots, lanes = cells.shape
    return pl.pallas_call(
        read_kernel,
        grid=(slots // GROUP,),
        in_specs=[
            pl.BlockSpec((GROUP, lanes), lambda i: (i, 0)),
            pl.BlockSpec(half.shape, lambda i: (0, 0)),
        ],
        out_specs=pl.BlockSpec((GROUP, samples, lanes), lambda i: (i, 0, 0)),
        out_shape=jax.ShapeDtypeStruct((slots, samples, lanes), BF),
        scratch_shapes=[pltpu.VMEM((LOW, GROUP * lanes), BF)],
        cost_estimate=pl.CostEstimate(
            flops=2 * slots * lanes * half.size,
            bytes_accessed=slots * lanes * samples * 2,
            transcendentals=0,
        ),
        name="read",
    )(cells, half)


def adjoint_kernel(blocks, block_rows, cells, back0, back1, filt, mats, out, acc):
    nblk, samples, lanes = filt.shape
    tiles = back0.shape[0]
    per = nblk // mats.shape[0]
    step = pl.program_id(0)

    @pl.when(step == 0)
    def _():
        slots = cells.shape[0]
        live = (cells[...] >= 0).astype(F32).astype(BF)
        ids = lax.broadcasted_iota(jnp.int32, (64, slots), 0)
        pick = (ids == block_rows[...]).astype(F32).astype(BF)
        count = jnp.dot(pick, live, preferred_element_type=F32)
        for b in range(nblk):
            acc[b] = filt[b].astype(F32) * count[b : b + 1, :]

    for k in range(tiles):
        d = step * tiles + k
        b0 = blocks[2 * d]
        acc[b0] = acc[b0] - back0[k].astype(F32)
        b1 = blocks[2 * d + 1]
        acc[b1] = acc[b1] - back1[k].astype(F32)

    @pl.when(step == pl.num_programs(0) - 1)
    def _():
        for b in range(nblk):
            out[b * lanes : (b + 1) * lanes, :] = lax.dot_general(
                acc[b].astype(BF),
                mats[b // per],
                (((0,), (0,)), ((), ())),
                preferred_element_type=F32,
            )


def adjoint(blocks, cells, back0, back1, filt, mats):
    tiles = 8
    devices, samples, lanes = back0.shape
    nblk = filt.shape[0]
    full = lambda *shape: pl.BlockSpec(shape, lambda i, *_: (0,) * len(shape))
    back = pl.BlockSpec((tiles, samples, lanes), lambda i, *_: (i, 0, 0))
    return pl.pallas_call(
        adjoint_kernel,
        grid_spec=pltpu.PrefetchScalarGridSpec(
            num_scalar_prefetch=1,
            grid=(devices // tiles,),
            in_specs=[
                full(1, blocks.shape[0]),
                full(*cells.shape),
                back,
                back,
                full(*filt.shape),
                full(*mats.shape),
            ],
            out_specs=full(nblk * lanes, samples),
            scratch_shapes=[pltpu.VMEM((nblk, samples, lanes), F32)],
        ),
        out_shape=jax.ShapeDtypeStruct((nblk * lanes, samples), F32),
        name="adjoint",
    )(blocks, blocks[None, :], cells, back0, back1, filt, mats)


def with_halo(block, sides, width):
    for axis, dim in sides:
        count = lax.axis_size(axis)
        forward = [(i, i + 1) for i in range(count - 1)]
        backward = [(target, source) for source, target in forward]
        low = lax.ppermute(
            lax.slice_in_dim(block, block.shape[dim] - width, None, axis=dim), axis, forward
        )
        high = lax.ppermute(lax.slice_in_dim(block, 0, width, axis=dim), axis, backward)
        block = jnp.concatenate([low, block, high], axis=dim)
    return block


def cycle_box(values, rows_out, cols_out):
    box_total = jnp.zeros((rows_out, cols_out, values.shape[2]), F32)
    for row_shift in range(3):
        for col_shift in range(3):
            box_total = (
                box_total
                + values[row_shift : row_shift + rows_out, col_shift : col_shift + cols_out]
            )
    return box_total / 9.0


def tensor(tile_image):
    count_il = lax.axis_size("il")
    count_xl = lax.axis_size("xl")
    padded = with_halo(tile_image, (("il", 0), ("xl", 1)), 2)
    padded_time = jnp.pad(padded, ((0, 0), (0, 0), (1, 1)))
    grad_il = (padded[2:, 1:-1] - padded[:-2, 1:-1]) * 0.5
    grad_xl = (padded[1:-1, 2:] - padded[1:-1, :-2]) * 0.5
    grad_time = (padded_time[1:-1, 1:-1, 2:] - padded_time[1:-1, 1:-1, :-2]) * 0.5
    rows_il = lax.axis_index("il") * CIL + jnp.arange(CIL + 2, dtype=jnp.int32) - 1
    rows_xl = lax.axis_index("xl") * CXL + jnp.arange(CXL + 2, dtype=jnp.int32) - 1
    inside_il = ((rows_il >= 0) & (rows_il < CIL * count_il)).astype(F32)
    inside_xl = ((rows_xl >= 0) & (rows_xl < CXL * count_xl)).astype(F32)
    cycle_mask = inside_il[:, None, None] * inside_xl[None, :, None]
    factor_pairs = (
        (grad_il, grad_il),
        (grad_xl, grad_xl),
        (grad_time, grad_time),
        (grad_il, grad_xl),
        (grad_il, grad_time),
        (grad_xl, grad_time),
    )
    return jnp.stack(
        [
            cycle_box(left_part * right_part * cycle_mask, CIL, CXL)
            for left_part, right_part in factor_pairs
        ]
    )


def local(traces, filter_taps, slot_block, slot_cells, pair_count):
    devices = lax.axis_size("il") * lax.axis_size("xl")
    samples = traces.shape[1]
    capacity = slot_block.shape[2]
    row_block = slot_cells.shape[3]
    surveys, taps = filter_taps.shape
    cell_count = CIL * CXL
    both = ("il", "xl")
    swap = functools.partial(
        lax.all_to_all, axis_name=both, split_axis=0, concat_axis=0, tiled=True
    )
    padded = jnp.pad(filter_taps, ((0, 0), (0, samples - taps)))
    rev = jnp.roll(padded[:, ::-1], 1, axis=1)
    blocks = slot_block[0].reshape(-1)
    slot_live = jnp.arange(capacity, dtype=jnp.int32)[None, :] < pair_count[0][:, None]
    out_cells = jnp.where(slot_live[:, :, None], slot_cells[0], -1)
    in_cells = swap(out_cells)
    out0, out1, filt, mats = prep(traces, rev, blocks, surveys, samples, devices)
    in0 = swap(out0)
    in1 = swap(out1)
    cells0 = in_cells[:, 0]
    cells1 = in_cells[:, 1]
    first = bin_first(cells0, in0, cell_count)
    half, image = bin_last(cells1, in1, first, cell_count)
    ans0 = read(cells0, half, samples)
    back0 = swap(ans0)
    ans1 = read(cells1, half, samples)
    back1 = swap(ans1)
    structure_tensor = tensor(image.reshape(CIL, CXL, samples))
    adjoint_traces = adjoint(
        blocks, out_cells.reshape(-1, row_block), back0, back1, filt, mats
    )
    return (structure_tensor, adjoint_traces)


def solution(mesh):
    return jax.shard_map(
        local,
        mesh=mesh,
        in_specs=(
            P(("il", "xl"), None),
            P(),
            P(("il", "xl"), None, None),
            P(("il", "xl"), None, None, None),
            P(("il", "xl"), None),
        ),
        out_specs=(P(None, "il", "xl", None), P(("il", "xl"), None)),
        check_vma=False,
    )
```

time: 533 us -> 329 us (0.62)
  matrix products: 123 us -> 0 us
  local copies, waits for them, and re-layouts: 108 us -> 3.96 us
  Pallas kernels: 0 us -> 94.8 us
  waiting for transfers between devices: 200 us -> 108 us
  blocking collectives: 0 us -> 59.3 us
  other arithmetic: 49.9 us -> 14.7 us
    dot_general x36 -> x0, matrix products: 123 us -> none  [the longest x16 55.1 us: read_group(): lax.dot_general(selector, image_half, (((0,), (0,)), ((), ())), preferred...]
    pallas_call x0 -> x6, Pallas kernels: none -> 94.8 us  [the longest x2 38 us: read(): pl.pallas_call(read_kernel, grid=(slots // GROUP,), in_specs=[pl.BlockSpe...]
    ppermute x2, waiting for transfers between devices: 96.6 us -> 5.1 us  [with_halo(): lax.ppermute(lax.slice_in_dim(block, 0, width, axis=dim), axis, backward)]
    gather x3 -> x0, local copies, waits for them, and re-layouts: 70.3 us -> none  [the longest x2 61.7 us: filter_matrices(): picked = filter_taps[:, jnp.clip(lag_table, 0, tap_count - 1)]]
    all_to_all x0 -> x1, blocking collectives: none -> 59.3 us  [local(): in0 = swap(out0)]
    all_to_all x3 -> x4, waiting for transfers between devices: 99.5 us -> 62.8 us  [the longest x1 32.7 us: local(): in1 = swap(out1)]
    ppermute x2, waiting for transfers between devices: 3.72 us -> 39.7 us  [with_halo(): lax.ppermute(lax.slice_in_dim(block, block.shape[dim] - width, None, axis...]
    reduce_sum x16 -> x0, other arithmetic: 21.1 us -> none  [add_group(): fold_counts = fold_counts + jnp.sum(selector, axis=1, dtype=jnp.float32)]
  transfers between devices with their start and end apart: 7 -> 8, of which waited for: 4 -> 4; matrix products, arithmetic and copies ran while one was open for 18% -> 5% of each run, Pallas kernels for 0% -> 14%
where the time goes in v1:
time: 329 us; the launch traced here: 327 us
  waiting for transfers between devices  108 us (33%)
  Pallas kernels  94.8 us (29%)
  blocking collectives  59.3 us (18%)
  starting transfers between devices  46.1 us (14%)
  other arithmetic  14.7 us (4%)
  local copies, waits for them, and re-layouts  3.96 us (1%)
    all_to_all x1, blocking collectives, local(): in0 = swap(out0)  59.3 us
    ppermute x2, waiting for transfers between devices, with_halo(): lax.ppermute(lax.slice_in_dim(block, block.shape[dim] - width, None, axis...  39.7 us
    pallas_call x2, Pallas kernels, read(): pl.pallas_call(read_kernel, grid=(slots // GROUP,), in_specs=[pl.BlockSpe...  38 us
    all_to_all x1, waiting for transfers between devices, local(): in1 = swap(out1)  32.7 us
    all_to_all x1, waiting for transfers between devices, local(): back0 = swap(ans0)  30.1 us
    pallas_call x1, Pallas kernels, bin_last(): pl.pallas_call(bin_last_kernel, grid=(steps,), in_specs=[cells_spec, data...  16.4 us
    pallas_call x1, Pallas kernels, bin_first(): pl.pallas_call(bin_first_kernel, grid=(steps,), in_specs=[cells_spec, dat...  15.6 us
    pallas_call x1, Pallas kernels, adjoint(): pl.pallas_call(adjoint_kernel, grid_spec=pltpu.PrefetchScalarGridSpec(num...  14.1 us
  transfers between devices with their start and end apart: 8, of which 4 were waited for; matrix products, arithmetic and copies ran while one was open for 5% of the time, Pallas kernels for 14%

profile of v1, /device:TPU:62, one launch (start us, length us, event | category | flops | bytes accessed | tf_op | source)
XLA Modules:
  0.0 327.2 jit_solution(6625020224415192349)
XLA Ops:
  0.6 0.7 iota_compare_fusion
  1.4 1.8 bitcast_select_fusion
  3.1 10.0 %all-to-all-start = ((s32[128,2,128]{2,1,0:T(2,128)}), s32[128,2,128]{2,1,0:T(2,128)S(1)}, u32[]{:S(2)}, u32[]{:S(2)}) async-start(s32[128,2,128]{2,1,0:T(2,128)} %bitcast_select_fusion), calls=%async_computation | async-start | bytes 262144 | tf_op jit(solution)/shard_map/all_to_all | solution.py:360
  13.2 0.8 pad_slice_fusion.2
  14.0 0.8 copy.14
  14.8 0.7 reshape_squeeze.3.blocks
  15.5 0.1 slice.222
  15.6 1.4 pad_maximum_fusion.10.rev
  16.9 10.6 %prep.1 = (bf16[128,128,128]{2,1,0:T(8,128)(2,1)}, bf16[128,128,128]{2,1,0:T(8,128)(2,1)}, bf16[60,128,128]{2,1,0:T(8,128)(2,1)}, bf16[12,128,128]{2,1,0:T(8,128)(2,1)}) custom-call(s32[256]{0:T(256)} %reshape_squeeze.3.blocks, bf16[7680,128]{1,0:T(8,128)(2,1)} %traces.1, f32[12,128]{1,0:T(8,128)} %pad_maximum_fusion.10.rev), custom_call_target="tpu_custom_call" | custom-call | tf_op jit(solution)/shard_map/prep/pallas_call | solution.py:55
  27.5 0.0 all-to-all-done
  27.5 59.3 %all_to_all.25.data = bf16[128,128,128]{2,1,0:T(8,128)(2,1)} all-to-all(bf16[128,128,128]{2,1,0:T(8,128)(2,1)} %get-tuple-element.9), channel_id=1, replica_groups=mesh['il'=8,'xl'=16] {'il','xl'}, dimensions={0} | all-to-all | bytes 8388608 | tf_op jit(solution)/shard_map/all_to_all | solution.py:362
  86.9 8.0 %all-to-all-start.1 = ((bf16[128,128,128]{2,1,0:T(8,128)(2,1)}), bf16[128,128,128]{2,1,0:T(8,128)(2,1)}, u32[]{:S(2)}, u32[]{:S(2)}) async-start(bf16[128,128,128]{2,1,0:T(8,128)(2,1)} %get-tuple-element.8), calls=%async_computation.1 | async-start | bytes 8388608 | tf_op jit(solution)/shard_map/all_to_all | solution.py:363
  94.9 0.8 fusion.24
  95.7 15.6 %bin_first.1.before = f32[784,256]{1,0:T(8,128)} custom-call(s32[128,128]{1,0:T(8,128)} %bitcast.45, bf16[128,128,128]{2,1,0:T(8,128)(2,1)} %all_to_all.25.data), custom_call_target="tpu_custom_call" | custom-call | flops 6576668672 | bytes 4194304 | tf_op jit(solution)/shard_map/bin_first/pallas_call | solution.py:144
  111.3 32.7 %all-to-all-done.1.data = bf16[128,128,128]{2,1,0:T(8,128)(2,1)} async-done(((bf16[128,128,128]{2,1,0:T(8,128)(2,1)}), bf16[128,128,128]{2,1,0:T(8,128)(2,1)}, u32[]{:S(2)}, u32[]{:S(2)}) %all-to-all-start.1) | async-done | bytes 4194336 | tf_op jit(solution)/shard_map/all_to_all | solution.py:363
  144.0 16.4 %bin_last.1 = (bf16[768,256]{1,0:T(8,128)(2,1)}, f32[1536,128]{1,0:T(8,128)}) custom-call(s32[128,128]{1,0:T(8,128)} %bitcast.43, bf16[128,128,128]{2,1,0:T(8,128)(2,1)} %all-to-all-done.1.data, f32[784,256]{1,0:T(8,128)} %bin_first.1.before), custom_call_target="tpu_custom_call" | custom-call | flops 6576668672 | bytes 4194304 | tf_op jit(solution)/shard_map/bin_last/pallas_call | solution.py:167
  160.4 19.0 %read.2 = bf16[128,128,128]{2,1,0:T(8,128)(2,1)} custom-call(s32[128,128]{1,0:T(8,128)} %bitcast.46, bf16[768,256]{1,0:T(8,128)(2,1)} %get-tuple-element.11.half), custom_call_target="tpu_custom_call" | custom-call | flops 6442450944 | bytes 4194304 | tf_op jit(solution)/shard_map/read/pallas_call | solution.py:211
  179.4 8.0 %all-to-all-start.3 = ((bf16[128,128,128]{2,1,0:T(8,128)(2,1)}), bf16[128,128,128]{2,1,0:T(8,128)(2,1)}, u32[]{:S(2)}, u32[]{:S(2)}) async-start(bf16[128,128,128]{2,1,0:T(8,128)(2,1)} %read.2), calls=%async_computation.3 | async-start | bytes 8388608 | tf_op jit(solution)/shard_map/all_to_all | solution.py:369
  187.4 19.0 %read.3 = bf16[128,128,128]{2,1,0:T(8,128)(2,1)} custom-call(s32[128,128]{1,0:T(8,128)} %bitcast.44, bf16[768,256]{1,0:T(8,128)(2,1)} %get-tuple-element.11.half), custom_call_target="tpu_custom_call" | custom-call | flops 6442450944 | bytes 4194304 | tf_op jit(solution)/shard_map/read/pallas_call | solution.py:211
  206.4 0.0 copy-start.1
  206.4 0.0 copy-start
  206.4 30.1 %all-to-all-done.3.back0 = bf16[128,128,128]{2,1,0:T(8,128)(2,1)} async-done(((bf16[128,128,128]{2,1,0:T(8,128)(2,1)}), bf16[128,128,128]{2,1,0:T(8,128)(2,1)}, u32[]{:S(2)}, u32[]{:S(2)}) %all-to-all-start.3) | async-done | bytes 4194336 | tf_op jit(solution)/shard_map/all_to_all | solution.py:369
  236.5 8.0 %all-to-all-start.4 = ((bf16[128,128,128]{2,1,0:T(8,128)(2,1)}), bf16[128,128,128]{2,1,0:T(8,128)(2,1)}, u32[]{:S(2)}, u32[]{:S(2)}) async-start(bf16[128,128,128]{2,1,0:T(8,128)(2,1)} %read.3), calls=%async_computation.4 | async-start | bytes 8388608 | tf_op jit(solution)/shard_map/all_to_all | solution.py:371
  244.5 0.1 lt.51
  244.7 0.0 copy-done.1
  244.7 0.7 broadcast_select_fusion.cells
  245.4 0.0 copy-done
  245.5 2.1 collective-permute-start
  247.5 3.5 %collective-permute-start.1 = (f32[2,48,128]{2,1,0:T(8,128)S(1)}, f32[2,48,128]{2,1,0:T(8,128)S(1)}, u32[]{:S(2)}, u32[]{:S(2)}) collective-permute-start(f32[2,48,128]{2,1,0:T(8,128)S(1)} %bitcast.47), channel_id=1, source_target_pairs={{16,0},{32,16},{48,32},{64,48},{80,64},{96,80},{112,96},{17,1},{33... | collective-permute-start | bytes 147464 | tf_op jit(solution)/shard_map/ppermute | solution.py:299
  251.0 39.7 %collective-permute-done = f32[2,48,128]{2,1,0:T(8,128)S(1)} collective-permute-done((f32[2,48,128]{2,1,0:T(8,128)S(1)}, f32[2,48,128]{2,1,0:T(8,128)S(1)}, u32[]{:S(2)}, u32[]{:S(2)}) %collective-permute-start) | collective-permute-done | bytes 49184 | tf_op jit(solution)/shard_map/ppermute | solution.py:296
  290.7 0.0 collective-permute-done.1
  290.7 4.4 %collective-permute-start.2 = (f32[36,2,128]{2,1,0:T(2,128)S(1)}, f32[36,2,128]{2,1,0:T(2,128)S(1)}, u32[]{:S(2)}, u32[]{:S(2)}) collective-permute-start(f32[36,2,128]{2,1,0:T(2,128)S(1)} %get-tuple-element.20), channel_id=1, source_target_pairs={{0,1},{1,2},{2,3},{3,4},{4,5},{5,6},{6,7},{7,8},{8,9},{9,10},{10,1... | collective-permute-start | bytes 110600 | tf_op jit(solution)/shard_map/ppermute | solution.py:296
  295.1 2.1 collective-permute-start.3
  297.2 0.1 broadcast_multiply_fusion
  297.3 0.7 broadcast_in_dim_reshape_squeeze.3.block_rows
  298.0 0.0 collective-permute-done.2
  298.0 5.1 %collective-permute-done.3 = f32[36,2,128]{2,1,0:T(2,128)S(1)} collective-permute-done((f32[36,2,128]{2,1,0:T(2,128)S(1)}, f32[36,2,128]{2,1,0:T(2,128)S(1)}, u32[]{:S(2)}, u32[]{:S(2)}) %collective-permute-start.3) | collective-permute-done | bytes 36896 | tf_op jit(solution)/shard_map/ppermute | solution.py:299
  303.1 0.1 pad_maximum_fusion
  303.2 2.1 multiply_multiply_fusion
  305.3 1.2 fusion.22
  306.5 0.4 multiply_multiply_fusion.2
  306.9 1.2 fusion.19
  308.2 1.2 fusion.16
  309.4 1.2 fusion.13
  310.6 1.2 fusion.10
  311.8 1.2 fusion.7
  313.1 0.0 all-to-all-done.4.back1
  313.1 14.1 %adjoint.1 = f32[7680,128]{1,0:T(8,128)} custom-call(s32[256]{0:T(256)} %reshape_squeeze.3.blocks, s32[1,256]{1,0:T(1,128)} %broadcast_in_dim_reshape_squeeze.3.block_rows, s32[256,128]{1,0:T(8,128)} %broadcast_select_fusion.cells, bf16[128,128,128]{2,1,0:T(8,128)(2,1)} %all-to-all-done.3.back0, bf16[128,128,128]{2,1,0:T(8,128)(2,1)} %all-to-all-done.4.back1, ...), custom_call_target="tpu_custom_call" | custom-call | tf_op jit(solution)/shard_map/adjoint/pallas_call | solution.py:270
  (4 shorter events, 0.0 us)
Async XLA Ops:
  3.1 24.4 %all-to-all-start = ((s32[128,2,128]{2,1,0:T(2,128)}), s32[128,2,128]{2,1,0:T(2,128)S(1)}, u32[]{:S(2)}, u32[]{:S(2)}) async-start(s32[128,2,128]{2,1,0:T(2,128)} %bitcast_select_fusion), calls=%async_computation | async-start | bytes 262144 | tf_op jit(solution)/shard_map/all_to_all | solution.py:360
  86.9 57.1 %all-to-all-start.1 = ((bf16[128,128,128]{2,1,0:T(8,128)(2,1)}), bf16[128,128,128]{2,1,0:T(8,128)(2,1)}, u32[]{:S(2)}, u32[]{:S(2)}) async-start(bf16[128,128,128]{2,1,0:T(8,128)(2,1)} %get-tuple-element.8), calls=%async_computation.1 | async-start | bytes 8388608 | tf_op jit(solution)/shard_map/all_to_all | solution.py:363
  179.4 57.1 %all-to-all-start.3 = ((bf16[128,128,128]{2,1,0:T(8,128)(2,1)}), bf16[128,128,128]{2,1,0:T(8,128)(2,1)}, u32[]{:S(2)}, u32[]{:S(2)}) async-start(bf16[128,128,128]{2,1,0:T(8,128)(2,1)} %read.2), calls=%async_computation.3 | async-start | bytes 8388608 | tf_op jit(solution)/shard_map/all_to_all | solution.py:369
  206.4 38.3 %copy-start.1 = (s32[1,128,2,128]{3,2,1,0:T(2,128)S(1)}, s32[1,128,2,128]{3,2,1,0:T(2,128)}, u32[]{:S(2)}) copy-start(s32[1,128,2,128]{3,2,1,0:T(2,128)} %param.8) | copy-start | bytes 393220
  206.4 39.0 %copy-start = (f32[1536,128]{1,0:T(8,128)S(1)}, f32[1536,128]{1,0:T(8,128)}, u32[]{:S(2)}) copy-start(f32[1536,128]{1,0:T(8,128)} %get-tuple-element.10) | copy-start | bytes 2359300
  236.5 76.5 %all-to-all-start.4 = ((bf16[128,128,128]{2,1,0:T(8,128)(2,1)}), bf16[128,128,128]{2,1,0:T(8,128)(2,1)}, u32[]{:S(2)}, u32[]{:S(2)}) async-start(bf16[128,128,128]{2,1,0:T(8,128)(2,1)} %read.3), calls=%async_computation.4 | async-start | bytes 8388608 | tf_op jit(solution)/shard_map/all_to_all | solution.py:371
  245.5 45.2 %collective-permute-start = (f32[2,48,128]{2,1,0:T(8,128)S(1)}, f32[2,48,128]{2,1,0:T(8,128)S(1)}, u32[]{:S(2)}, u32[]{:S(2)}) collective-permute-start(f32[2,48,128]{2,1,0:T(8,128)S(1)} %bitcast.48), channel_id=1, source_target_pairs={{0,16},{16,32},{32,48},{48,64},{64,80},{80,96},{96,112},{1,17},{17... | collective-permute-start | bytes 147464 | tf_op jit(solution)/shard_map/ppermute | solution.py:296
  247.5 43.2 %collective-permute-start.1 = (f32[2,48,128]{2,1,0:T(8,128)S(1)}, f32[2,48,128]{2,1,0:T(8,128)S(1)}, u32[]{:S(2)}, u32[]{:S(2)}) collective-permute-start(f32[2,48,128]{2,1,0:T(8,128)S(1)} %bitcast.47), channel_id=1, source_target_pairs={{16,0},{32,16},{48,32},{64,48},{80,64},{96,80},{112,96},{17,1},{33... | collective-permute-start | bytes 147464 | tf_op jit(solution)/shard_map/ppermute | solution.py:299
  290.7 7.3 %collective-permute-start.2 = (f32[36,2,128]{2,1,0:T(2,128)S(1)}, f32[36,2,128]{2,1,0:T(2,128)S(1)}, u32[]{:S(2)}, u32[]{:S(2)}) collective-permute-start(f32[36,2,128]{2,1,0:T(2,128)S(1)} %get-tuple-element.20), channel_id=1, source_target_pairs={{0,1},{1,2},{2,3},{3,4},{4,5},{5,6},{6,7},{7,8},{8,9},{9,10},{10,1... | collective-permute-start | bytes 110600 | tf_op jit(solution)/shard_map/ppermute | solution.py:296
  295.1 8.0 %collective-permute-start.3 = (f32[36,2,128]{2,1,0:T(2,128)S(1)}, f32[36,2,128]{2,1,0:T(2,128)S(1)}, u32[]{:S(2)}, u32[]{:S(2)}) collective-permute-start(f32[36,2,128]{2,1,0:T(2,128)S(1)} %get-tuple-element.21), channel_id=1, source_target_pairs={{1,0},{2,1},{3,2},{4,3},{5,4},{6,5},{7,6},{8,7},{9,8},{10,9},{11,1... | collective-permute-start | bytes 110600 | tf_op jit(solution)/shard_map/ppermute | solution.py:299

commit v2 on v1

v2 whole, which is shorter than its diff:
```python
import functools

import jax
import jax.numpy as jnp
from jax import lax
from jax.experimental import pallas as pl
from jax.experimental.pallas import tpu as pltpu
from jax.sharding import PartitionSpec as P

CIL = 32
CXL = 48
LOW = 256
GROUP = 8
BF = jnp.bfloat16
F32 = jnp.float32


def prep_kernel(blocks, traces, rev, cells, out, filt, mats):
    surveys = mats.shape[0]
    samples = mats.shape[1]
    rows = traces.shape[0] // surveys
    per = rows // samples
    tiles, slots = cells.shape[:2]
    part = samples // 2
    step = pl.program_id(0)

    @pl.when(step == 0)
    def _():
        t_id = lax.broadcasted_iota(jnp.int32, (samples, samples), 0)
        u_id = lax.broadcasted_iota(jnp.int32, (samples, samples), 1)
        for s in range(surveys):
            base = jnp.broadcast_to(rev[s : s + 1, :], (samples, samples))
            skew = pltpu.roll(base, 0, 1, stride=1, stride_axis=0)
            mat = jnp.where(u_id <= t_id, skew, 0.0).astype(BF)
            mats[s] = mat
            res = lax.dot_general(
                mat,
                traces[s * rows : (s + 1) * rows, :],
                (((1,), (1,)), ((), ())),
                preferred_element_type=F32,
            ).astype(BF)
            for b in range(per):
                filt[s * per + b] = res[:, b * samples : (b + 1) * samples]

    for k in range(tiles):
        for c in range(slots):
            block = blocks[(step * tiles + k) * slots + c]
            out[k, c * part : (c + 1) * part, :] = filt[block, :part, :]
        here = cells[k]
        tags = [here & (LOW - 1), here >> 8, jnp.zeros((8 - 2 * slots, samples), jnp.int32)]
        out[k, slots * part :, :] = jnp.concatenate(tags, axis=0).astype(F32).astype(BF)


def prep(traces, rev, blocks, cells, surveys):
    tiles = 8
    devices, slots, samples = cells.shape
    nblk = traces.shape[0] // samples
    part = samples // 2
    full = lambda *shape: pl.BlockSpec(shape, lambda i, *_: (0,) * len(shape))
    return pl.pallas_call(
        prep_kernel,
        grid_spec=pltpu.PrefetchScalarGridSpec(
            num_scalar_prefetch=1,
            grid=(devices // tiles,),
            in_specs=[
                full(*traces.shape),
                full(*rev.shape),
                pl.BlockSpec((tiles, slots, samples), lambda i, *_: (i, 0, 0)),
            ],
            out_specs=[
                pl.BlockSpec((tiles, slots * part + 8, samples), lambda i, *_: (i, 0, 0)),
                full(nblk, samples, samples),
                full(surveys, samples, samples),
            ],
        ),
        out_shape=[
            jax.ShapeDtypeStruct((devices, slots * part + 8, samples), BF),
            jax.ShapeDtypeStruct((nblk, samples, samples), BF),
            jax.ShapeDtypeStruct((surveys, samples, samples), BF),
        ],
        name="prep",
    )(blocks, traces, rev, cells)


def late_kernel(blocks, filt, out):
    tiles, slots, part = out.shape[:3]
    step = pl.program_id(0)
    for k in range(tiles):
        for c in range(slots):
            out[k, c] = filt[blocks[(step * tiles + k) * slots + c], part:, :]


def late(blocks, filt, devices, slots):
    tiles = 8
    nblk, samples, lanes = filt.shape
    part = samples // 2
    return pl.pallas_call(
        late_kernel,
        grid_spec=pltpu.PrefetchScalarGridSpec(
            num_scalar_prefetch=1,
            grid=(devices // tiles,),
            in_specs=[pl.BlockSpec(filt.shape, lambda i, *_: (0, 0, 0))],
            out_specs=pl.BlockSpec((tiles, slots, part, lanes), lambda i, *_: (i, 0, 0, 0)),
        ),
        out_shape=jax.ShapeDtypeStruct((devices, slots, part, lanes), BF),
        cost_estimate=pl.CostEstimate(
            flops=0, bytes_accessed=filt.size * 2 + devices * slots * part * lanes * 2,
            transcendentals=0,
        ),
        name="late",
    )(blocks, filt)


def low_hot(cells, lanes):
    ids = lax.broadcasted_iota(jnp.int32, (LOW, lanes), 0)
    return (ids == (cells & (LOW - 1))).astype(F32).astype(BF)


def fill(cells, pick, samples, left, hot):
    group, lanes = cells.shape
    highs = (left.shape[0] - 16) // samples
    ids = lax.broadcasted_iota(jnp.int32, (16, lanes), 0)
    for g in range(group):
        at = slice(g * lanes, (g + 1) * lanes)
        here = cells[g : g + 1, :]
        high = here >> 8
        hot[:, at] = low_hot(here, lanes)
        block = pick(g)
        masks = (ids == high).astype(F32).astype(BF)
        left[highs * samples :, at] = masks
        for h in range(highs):
            left[h * samples : (h + 1) * samples, at] = block * jnp.broadcast_to(
                (high == h).astype(F32).astype(BF), block.shape
            )


def accumulate(cells, pick, part, acc, left, hot):
    @pl.when(pl.program_id(0) == 0)
    def _():
        acc[...] = jnp.zeros_like(acc)

    fill(cells, pick, part, left, hot)
    acc[...] += lax.dot_general(
        left[...], hot[...], (((1,), (1,)), ((), ())), preferred_element_type=F32
    )


def divided(acc, h, part, highs):
    fold = acc[highs * part + h : highs * part + h + 1, :]
    return acc[h * part : (h + 1) * part, :] / jnp.maximum(fold, 1.0)


def bin_early_kernel(cells, data, half, value, acc, left, hot):
    slots = cells.shape[0] // data.shape[0]
    part = data.shape[1] // slots // 16 * 16

    def pick(g):
        return data[g // slots, g % slots * part : (g % slots + 1) * part, :]

    accumulate(cells, pick, part, acc, left, hot)

    @pl.when(pl.program_id(0) == pl.num_programs(0) - 1)
    def _():
        highs = half.shape[0] // part
        for h in range(highs):
            at = slice(h * part, (h + 1) * part)
            mean = divided(acc, h, part, highs)
            half[at, :] = mean.astype(BF)
            value[at, :] = mean


def bin_late_kernel(cells, data, value, half, image, acc, left, hot):
    part = data.shape[1]
    accumulate(cells, lambda g: data[g], part, acc, left, hot)

    @pl.when(pl.program_id(0) == pl.num_programs(0) - 1)
    def _():
        highs = half.shape[0] // part
        for h in range(highs):
            at = slice(h * part, (h + 1) * part)
            mean = divided(acc, h, part, highs)
            half[at, :] = mean.astype(BF)
            image[h * LOW : (h + 1) * LOW, :] = jnp.concatenate([value[at, :], mean], axis=0).T


def binned(kernel, cells, data, extra, out, name, cell_count):
    slots, lanes = cells.shape
    step = GROUP * data.shape[0] // slots
    part = data.shape[0] * data.shape[1] // slots // 16 * 16
    rows = cell_count // LOW * part
    tall = rows + 16
    whole = lambda shape: pl.BlockSpec(shape, lambda i: (0,) * len(shape))
    return pl.pallas_call(
        kernel,
        grid=(slots // GROUP,),
        in_specs=[
            pl.BlockSpec((GROUP, lanes), lambda i: (i, 0)),
            pl.BlockSpec((step, data.shape[1], lanes), lambda i: (i, 0, 0)),
        ]
        + [whole(x.shape) for x in extra],
        out_specs=[whole((rows, LOW)), whole(out)],
        out_shape=[jax.ShapeDtypeStruct((rows, LOW), BF), jax.ShapeDtypeStruct(out, F32)],
        scratch_shapes=[
            pltpu.VMEM((tall, LOW), F32),
            pltpu.VMEM((tall, GROUP * lanes), BF),
            pltpu.VMEM((LOW, GROUP * lanes), BF),
        ],
        cost_estimate=pl.CostEstimate(
            flops=2 * slots * lanes * tall * LOW, bytes_accessed=data.size * 2, transcendentals=0
        ),
        name=name,
    )(cells, data, *extra)


def read_kernel(cells, half, out, hot):
    group, part, lanes = out.shape
    highs = half.shape[0] // part
    for g in range(group):
        hot[:, g * lanes : (g + 1) * lanes] = low_hot(cells[g : g + 1, :], lanes)
    for pair in range(group // 2):
        wide = jnp.dot(
            half[...],
            hot[:, 2 * pair * lanes : 2 * (pair + 1) * lanes],
            preferred_element_type=F32,
        )
        for k in range(2):
            g = 2 * pair + k
            mine = wide[:, k * lanes : (k + 1) * lanes]
            high = jnp.broadcast_to(cells[g : g + 1, :] >> 8, (part, lanes))
            picked = jnp.zeros((part, lanes), F32)
            for h in range(highs):
                picked = jnp.where(high == h, mine[h * part : (h + 1) * part, :], picked)
            out[g] = picked.astype(BF)


def read(cells, half, part, name):
    slots, lanes = cells.shape
    return pl.pallas_call(
        read_kernel,
        grid=(slots // GROUP,),
        in_specs=[
            pl.BlockSpec((GROUP, lanes), lambda i: (i, 0)),
            pl.BlockSpec(half.shape, lambda i: (0, 0)),
        ],
        out_specs=pl.BlockSpec((GROUP, part, lanes), lambda i: (i, 0, 0)),
        out_shape=jax.ShapeDtypeStruct((slots, part, lanes), BF),
        scratch_shapes=[pltpu.VMEM((LOW, GROUP * lanes), BF)],
        cost_estimate=pl.CostEstimate(
            flops=2 * slots * lanes * half.size,
            bytes_accessed=slots * lanes * part * 2,
            transcendentals=0,
        ),
        name=name,
    )(cells, half)


def subtract(first, blocks, block_rows, cells, back, filt, acc):
    nblk, part = acc.shape[:2]
    tiles, slots = back.shape[:2]
    step = pl.program_id(0)

    @pl.when(step == 0)
    def _():
        live = (cells[...] >= 0).astype(F32).astype(BF)
        ids = lax.broadcasted_iota(jnp.int32, (64, cells.shape[0]), 0)
        pick = (ids == block_rows[...]).astype(F32).astype(BF)
        count = jnp.dot(pick, live, preferred_element_type=F32)
        for b in range(nblk):
            acc[b] = filt[b, first : first + part, :].astype(F32) * count[b : b + 1, :]

    for k in range(tiles):
        for c in range(slots):
            b = blocks[(step * tiles + k) * slots + c]
            acc[b] = acc[b] - back[k, c].astype(F32)


def misfit_kernel(blocks, block_rows, cells, back, filt, out, acc):
    subtract(0, blocks, block_rows, cells, back, filt, acc)

    @pl.when(pl.program_id(0) == pl.num_programs(0) - 1)
    def _():
        out[...] = acc[...].astype(BF)


def adjoint_kernel(blocks, block_rows, cells, back, filt, early, mats, out, acc):
    nblk, part, lanes = acc.shape
    subtract(part, blocks, block_rows, cells, back, filt, acc)
    per = nblk // mats.shape[0]

    @pl.when(pl.program_id(0) == pl.num_programs(0) - 1)
    def _():
        for b in range(nblk):
            out[b * lanes : (b + 1) * lanes, :] = lax.dot_general(
                jnp.concatenate([early[b], acc[b].astype(BF)], axis=0),
                mats[b // per],
                (((0,), (0,)), ((), ())),
                preferred_element_type=F32,
            )


def owner_call(kernel, blocks, cells, back, rest, out_shape, name):
    tiles = 8
    devices, slots, part, lanes = back.shape
    nblk = rest[0].shape[0]
    full = lambda *shape: pl.BlockSpec(shape, lambda i, *_: (0,) * len(shape))
    return pl.pallas_call(
        kernel,
        grid_spec=pltpu.PrefetchScalarGridSpec(
            num_scalar_prefetch=1,
            grid=(devices // tiles,),
            in_specs=[
                full(1, blocks.shape[0]),
                full(*cells.shape),
                pl.BlockSpec((tiles, slots, part, lanes), lambda i, *_: (i, 0, 0, 0)),
            ]
            + [full(*x.shape) for x in rest],
            out_specs=full(*out_shape.shape),
            scratch_shapes=[pltpu.VMEM((nblk, part, lanes), F32)],
        ),
        out_shape=out_shape,
        cost_estimate=pl.CostEstimate(
            flops=0, bytes_accessed=back.size * 2 + rest[0].size * 4, transcendentals=0
        ),
        name=name,
    )(blocks, blocks[None, :], cells, back, *rest)


def edges(block, axis, dim, width):
    count = lax.axis_size(axis)
    forward = [(i, i + 1) for i in range(count - 1)]
    backward = [(target, source) for source, target in forward]
    low = lax.ppermute(
        lax.slice_in_dim(block, block.shape[dim] - width, None, axis=dim), axis, forward
    )
    high = lax.ppermute(lax.slice_in_dim(block, 0, width, axis=dim), axis, backward)
    return low, high


def cycle_box(values, rows_out, cols_out):
    box_total = jnp.zeros((rows_out, cols_out, values.shape[2]), F32)
    for row_shift in range(3):
        for col_shift in range(3):
            box_total = (
                box_total
                + values[row_shift : row_shift + rows_out, col_shift : col_shift + cols_out]
            )
    return box_total / 9.0


def tensor(padded):
    count_il = lax.axis_size("il")
    count_xl = lax.axis_size("xl")
    padded_time = jnp.pad(padded, ((0, 0), (0, 0), (1, 1)))
    grad_il = (padded[2:, 1:-1] - padded[:-2, 1:-1]) * 0.5
    grad_xl = (padded[1:-1, 2:] - padded[1:-1, :-2]) * 0.5
    grad_time = (padded_time[1:-1, 1:-1, 2:] - padded_time[1:-1, 1:-1, :-2]) * 0.5
    rows_il = lax.axis_index("il") * CIL + jnp.arange(CIL + 2, dtype=jnp.int32) - 1
    rows_xl = lax.axis_index("xl") * CXL + jnp.arange(CXL + 2, dtype=jnp.int32) - 1
    inside_il = ((rows_il >= 0) & (rows_il < CIL * count_il)).astype(F32)
    inside_xl = ((rows_xl >= 0) & (rows_xl < CXL * count_xl)).astype(F32)
    cycle_mask = inside_il[:, None, None] * inside_xl[None, :, None]
    factor_pairs = (
        (grad_il, grad_il),
        (grad_xl, grad_xl),
        (grad_time, grad_time),
        (grad_il, grad_xl),
        (grad_il, grad_time),
        (grad_xl, grad_time),
    )
    return jnp.stack(
        [
            cycle_box(left_part * right_part * cycle_mask, CIL, CXL)
            for left_part, right_part in factor_pairs
        ]
    )


def local(traces, filter_taps, slot_block, slot_cells, pair_count):
    devices = lax.axis_size("il") * lax.axis_size("xl")
    rows, samples = traces.shape
    slots = slot_block.shape[2]
    lanes = slot_cells.shape[3]
    surveys, taps = filter_taps.shape
    cell_count = CIL * CXL
    part = samples // 2
    flat = (devices * slots, part, lanes)
    boxed = (devices, slots, part, lanes)
    high_rows = cell_count // LOW * part
    swap = functools.partial(
        lax.all_to_all, axis_name=("il", "xl"), split_axis=0, concat_axis=0, tiled=True
    )
    wide = jnp.pad(filter_taps, ((0, 0), (0, samples - taps)))
    rev = jnp.roll(wide[:, ::-1], 1, axis=1)
    blocks = slot_block[0].reshape(-1)
    slot_live = jnp.arange(slots, dtype=jnp.int32)[None, :] < pair_count[0][:, None]
    out_cells = jnp.where(slot_live[:, :, None], slot_cells[0], -1)
    out_early, filt, mats = prep(traces, rev, blocks, out_cells, surveys)
    in_early = swap(out_early)
    out_late = late(blocks, filt, devices, slots)
    in_late = swap(out_late)
    tags = in_early[:, slots * part :, :].astype(jnp.int32)
    cells = (tags[:, slots : 2 * slots] * LOW + tags[:, :slots]).reshape(-1, lanes)
    half_early, value = binned(
        bin_early_kernel, cells, in_early, (), (high_rows, LOW), "bin_early", cell_count
    )
    answer_early = read(cells, half_early, part, "read_early")
    back_early = swap(answer_early.reshape(boxed))
    half_late, image = binned(
        bin_late_kernel,
        cells,
        in_late.reshape(flat),
        (value,),
        (cell_count, samples),
        "bin_late",
        cell_count,
    )
    answer_late = read(cells, half_late, part, "read_late")
    tile = image.reshape(CIL, CXL, samples)
    low, high = edges(tile, "il", 0, 2)
    answer_late, low, high = lax.optimization_barrier((answer_late, low, high))
    tall = jnp.concatenate([low, tile, high], axis=0)
    low, high = edges(tall, "xl", 1, 2)
    padded = jnp.concatenate([low, tall, high], axis=1)
    answer_late, padded = lax.optimization_barrier((answer_late, padded))
    back_late = swap(answer_late.reshape(boxed))
    structure_tensor = tensor(padded)
    mine = out_cells.reshape(-1, lanes)
    early = owner_call(
        misfit_kernel,
        blocks,
        mine,
        back_early,
        (filt,),
        jax.ShapeDtypeStruct((filt.shape[0], part, lanes), BF),
        "misfit",
    )
    adjoint_traces = owner_call(
        adjoint_kernel,
        blocks,
        mine,
        back_late,
        (filt, early, mats),
        jax.ShapeDtypeStruct((rows, samples), F32),
        "adjoint",
    )
    return (structure_tensor, adjoint_traces)


def solution(mesh):
    return jax.shard_map(
        local,
        mesh=mesh,
        in_specs=(
            P(("il", "xl"), None),
            P(),
            P(("il", "xl"), None, None),
            P(("il", "xl"), None, None, None),
            P(("il", "xl"), None),
        ),
        out_specs=(P(None, "il", "xl", None), P(("il", "xl"), None)),
        check_vma=False,
    )
```

time: 329 us -> 292 us (0.89)
  the two profiles are of different devices: /device:TPU:62 before, /device:TPU:7 now
where the time goes in v2:
time: 292 us; the launch traced here: 287 us
  Pallas kernels  137 us (47%)
  waiting for transfers between devices  84.2 us (29%)
  starting transfers between devices  45.4 us (16%)
  other arithmetic  15.9 us (5%)
  local copies, waits for them, and re-layouts  4.02 us (1%)
    pallas_call x2, Pallas kernels, binned(): pl.pallas_call(kernel, grid=(slots // GROUP,), in_specs=[pl.BlockSpec((GR...  50.9 us
    all_to_all x1, waiting for transfers between devices, local(): in_early = swap(out_early)  46.8 us
    pallas_call x2, Pallas kernels, read(): pl.pallas_call(read_kernel, grid=(slots // GROUP,), in_specs=[pl.BlockSpe...  41 us
    all_to_all x1, waiting for transfers between devices, local(): back_late = swap(answer_late.reshape(boxed))  29.4 us
    pallas_call x2, Pallas kernels, owner_call(): pl.pallas_call(kernel, grid_spec=pltpu.PrefetchScalarGridSpec(num_scalar_...  24.8 us
    all_to_all x1, starting transfers between devices, local(): back_late = swap(answer_late.reshape(boxed))  14.6 us
    pallas_call x1, Pallas kernels, prep(): pl.pallas_call(prep_kernel, grid_spec=pltpu.PrefetchScalarGridSpec(num_sc...  11.8 us
    all_to_all x1, starting transfers between devices, local(): in_early = swap(out_early)  11.2 us
  transfers between devices with their start and end apart: 8, of which 4 were waited for; matrix products, arithmetic and copies ran while one was open for 5% of the time, Pallas kernels for 39%

profile of v2, /device:TPU:7, one launch (start us, length us, event | category | flops | bytes accessed | tf_op | source)
XLA Modules:
  0.0 286.9 jit_solution(16275224728205192249)
XLA Ops:
  0.6 0.8 pad_slice_fusion.2
  1.4 0.1 slice.222
  1.5 0.7 iota_compare_fusion
  2.2 0.8 copy.8
  3.0 0.7 reshape_squeeze.3.blocks
  3.7 1.4 pad_maximum_fusion.4.rev
  5.1 1.8 bitcast_select_fusion.cells
  6.9 11.8 %prep.1 = (bf16[128,136,128]{2,1,0:T(8,128)(2,1)}, bf16[60,128,128]{2,1,0:T(8,128)(2,1)}, bf16[12,128,128]{2,1,0:T(8,128)(2,1)}) custom-call(s32[256]{0:T(256)} %reshape_squeeze.3.blocks, bf16[7680,128]{1,0:T(8,128)(2,1)} %traces.1, f32[12,128]{1,0:T(8,128)} %pad_maximum_fusion.4.rev, s32[128,2,128]{2,1,0:T(2,128)} %bitcast_select_fusion.cells), custom_call_target="tpu_custom_call" | custom-call | tf_op jit(solution)/shard_map/prep/pallas_call | solution.py:60
  18.7 11.2 %all-to-all-start = ((bf16[128,136,128]{2,1,0:T(8,128)(2,1)}), bf16[128,136,128]{2,1,0:T(8,128)(2,1)}, u32[]{:S(2)}, u32[]{:S(2)}) async-start(bf16[128,136,128]{2,1,0:T(8,128)(2,1)} %get-tuple-element.14), calls=%async_computation | async-start | bytes 8912896 | tf_op jit(solution)/shard_map/all_to_all | solution.py:398
  29.9 8.2 %late.1 = bf16[128,2,64,128]{3,2,1,0:T(8,128)(2,1)} custom-call(s32[256]{0:T(256)} %reshape_squeeze.3.blocks, bf16[60,128,128]{2,1,0:T(8,128)(2,1)} %get-tuple-element.15.filt), custom_call_target="tpu_custom_call" | custom-call | bytes 6160384 | tf_op jit(solution)/shard_map/late/pallas_call | solution.py:97
  38.1 46.8 %all-to-all-done.data = bf16[128,136,128]{2,1,0:T(8,128)(2,1)} async-done(((bf16[128,136,128]{2,1,0:T(8,128)(2,1)}), bf16[128,136,128]{2,1,0:T(8,128)(2,1)}, u32[]{:S(2)}, u32[]{:S(2)}) %all-to-all-start) | async-done | bytes 4456480 | tf_op jit(solution)/shard_map/all_to_all | solution.py:398
  84.9 5.3 %all-to-all-start.1 = ((bf16[128,2,64,128]{3,2,1,0:T(8,128)(2,1)}), bf16[128,2,64,128]{3,2,1,0:T(8,128)(2,1)}, u32[]{:S(2)}, u32[]{:S(2)}) async-start(bf16[128,2,64,128]{3,2,1,0:T(8,128)(2,1)} %late.1), calls=%async_computation.1 | async-start | bytes 8388608 | tf_op jit(solution)/shard_map/all_to_all | solution.py:400
  90.1 1.0 slice_convert_fusion
  91.1 0.7 slice_add_fusion.48
  91.9 25.2 %bin_early.1 = (bf16[384,256]{1,0:T(8,128)(2,1)}, f32[384,256]{1,0:T(8,128)}) custom-call(s32[256,128]{1,0:T(8,128)} %bitcast.41, bf16[128,136,128]{2,1,0:T(8,128)(2,1)} %all-to-all-done.data), custom_call_target="tpu_custom_call" | custom-call | flops 6710886400 | bytes 4456448 | tf_op jit(solution)/shard_map/bin_early/pallas_call | solution.py:193
  117.1 20.5 %read_early.1 = bf16[256,64,128]{2,1,0:T(8,128)(2,1)} custom-call(s32[256,128]{1,0:T(8,128)} %bitcast.42, bf16[384,256]{1,0:T(8,128)(2,1)} %get-tuple-element.24.half), custom_call_target="tpu_custom_call" | custom-call | flops 6442450944 | bytes 4194304 | tf_op jit(solution)/shard_map/read_early/pallas_call | solution.py:238
  137.6 4.5 %all-to-all-done.1 = bf16[128,2,64,128]{3,2,1,0:T(8,128)(2,1)} async-done(((bf16[128,2,64,128]{3,2,1,0:T(8,128)(2,1)}), bf16[128,2,64,128]{3,2,1,0:T(8,128)(2,1)}, u32[]{:S(2)}, u32[]{:S(2)}) %all-to-all-start.1) | async-done | bytes 4194336 | tf_op jit(solution)/shard_map/all_to_all | solution.py:400
  142.1 5.7 %all-to-all-start.3 = ((bf16[128,2,64,128]{3,2,1,0:T(8,128)(2,1)}), bf16[128,2,64,128]{3,2,1,0:T(8,128)(2,1)}, u32[]{:S(2)}, u32[]{:S(2)}) async-start(bf16[128,2,64,128]{3,2,1,0:T(8,128)(2,1)} %bitcast.37), calls=%async_computation.3 | async-start | bytes 8388608 | tf_op jit(solution)/shard_map/all_to_all | solution.py:407
  147.8 25.7 %bin_late.1 = (bf16[384,256]{1,0:T(8,128)(2,1)}, f32[1536,128]{1,0:T(8,128)}) custom-call(s32[256,128]{1,0:T(8,128)} %bitcast.43, bf16[256,64,128]{2,1,0:T(8,128)(2,1)} %bitcast.3.data, f32[384,256]{1,0:T(8,128)} %get-tuple-element.16.value), custom_call_target="tpu_custom_call" | custom-call | flops 6710886400 | bytes 4194304 | tf_op jit(solution)/shard_map/bin_late/pallas_call | solution.py:193
  173.5 0.8 fusion.20
  174.3 1.3 collective-permute-start
  175.6 3.0 %collective-permute-start.1 = (f32[2,48,128]{2,1,0:T(8,128)S(1)}, f32[2,48,128]{2,1,0:T(8,128)S(1)}, u32[]{:S(2)}, u32[]{:S(2)}) collective-permute-start(f32[2,48,128]{2,1,0:T(8,128)S(1)} %bitcast.45), channel_id=1, source_target_pairs={{16,0},{32,16},{48,32},{64,48},{80,64},{96,80},{112,96},{17,1},{33... | collective-permute-start | bytes 147464 | tf_op jit(solution)/shard_map/ppermute | solution.py:335
  178.6 0.0 copy-start
  178.7 20.5 %read_late.1 = bf16[256,64,128]{2,1,0:T(8,128)(2,1)} custom-call(s32[256,128]{1,0:T(8,128)} %bitcast.44, bf16[384,256]{1,0:T(8,128)(2,1)} %get-tuple-element.17.half), custom_call_target="tpu_custom_call" | custom-call | flops 6442450944 | bytes 4194304 | tf_op jit(solution)/shard_map/read_late/pallas_call | solution.py:238
  199.1 0.0 collective-permute-done
  199.1 0.0 collective-permute-done.1
  199.2 3.1 %collective-permute-start.2 = (f32[36,2,128]{2,1,0:T(2,128)S(1)}, f32[36,2,128]{2,1,0:T(2,128)S(1)}, u32[]{:S(2)}, u32[]{:S(2)}) collective-permute-start(f32[36,2,128]{2,1,0:T(2,128)S(1)} %get-tuple-element.32), channel_id=1, source_target_pairs={{0,1},{1,2},{2,3},{3,4},{4,5},{5,6},{6,7},{7,8},{8,9},{9,10},{10,1... | collective-permute-start | bytes 110600 | tf_op jit(solution)/shard_map/ppermute | solution.py:332
  202.3 1.3 collective-permute-start.3
  203.6 0.0 collective-permute-done.2
  203.6 3.4 %collective-permute-done.3 = f32[36,2,128]{2,1,0:T(2,128)S(1)} collective-permute-done((f32[36,2,128]{2,1,0:T(2,128)S(1)}, f32[36,2,128]{2,1,0:T(2,128)S(1)}, u32[]{:S(2)}, u32[]{:S(2)}) %collective-permute-start.3) | collective-permute-done | bytes 36896 | tf_op jit(solution)/shard_map/ppermute | solution.py:335
  207.0 0.1 pad_maximum_fusion
  207.1 0.0 copy-start.1
  207.1 0.0 all-to-all-done.3.back
  207.1 14.6 %all-to-all-start.2 = ((bf16[128,2,64,128]{3,2,1,0:T(8,128)(2,1)}), bf16[128,2,64,128]{3,2,1,0:T(8,128)(2,1)}, u32[]{:S(2)}, u32[]{:S(2)}) async-start(bf16[128,2,64,128]{3,2,1,0:T(8,128)(2,1)} %bitcast.36), calls=%async_computation.2 | async-start | bytes 8388608 | tf_op jit(solution)/shard_map/all_to_all | solution.py:425
  221.7 0.1 lt.51
  221.8 0.7 broadcast_in_dim_reshape_squeeze.4.block_rows
  222.5 0.1 broadcast_multiply_fusion
  222.6 0.8 broadcast_select_fusion.cells
  223.3 2.0 multiply_multiply_fusion
  225.4 1.2 fusion.19
  226.6 1.2 fusion.16
  227.8 1.2 fusion.13
  229.0 1.2 fusion.10
  230.2 1.2 fusion.7
  231.5 1.2 fusion.4
  232.7 11.5 %misfit.1.early = bf16[60,64,128]{2,1,0:T(8,128)(2,1)} custom-call(s32[256]{0:T(256)} %reshape_squeeze.3.blocks, s32[1,256]{1,0:T(1,128)} %broadcast_in_dim_reshape_squeeze.4.block_rows, s32[256,128]{1,0:T(8,128)} %broadcast_select_fusion.cells, bf16[128,2,64,128]{3,2,1,0:T(8,128)(2,1)} %all-to-all-done.3.back, bf16[60,128,128]{2,1,0:T(8,128)(2,1)} %get-tuple-element.15.filt), custom_call_target="tpu_custom_call" | custom-call | bytes 8126464 | tf_op jit(solution)/shard_map/misfit/pallas_call | solution.py:306
  244.2 29.4 %all-to-all-done.2.back = bf16[128,2,64,128]{3,2,1,0:T(8,128)(2,1)} async-done(((bf16[128,2,64,128]{3,2,1,0:T(8,128)(2,1)}), bf16[128,2,64,128]{3,2,1,0:T(8,128)(2,1)}, u32[]{:S(2)}, u32[]{:S(2)}) %all-to-all-start.2) | async-done | bytes 4194336 | tf_op jit(solution)/shard_map/all_to_all | solution.py:425
  273.6 13.3 %adjoint.1 = f32[7680,128]{1,0:T(8,128)} custom-call(s32[256]{0:T(256)} %reshape_squeeze.3.blocks, s32[1,256]{1,0:T(1,128)} %broadcast_in_dim_reshape_squeeze.4.block_rows, s32[256,128]{1,0:T(8,128)} %broadcast_select_fusion.cells, bf16[128,2,64,128]{3,2,1,0:T(8,128)(2,1)} %all-to-all-done.2.back, bf16[60,128,128]{2,1,0:T(8,128)(2,1)} %get-tuple-element.15.filt, ...), custom_call_target="tpu_custom_call" | custom-call | bytes 8126464 | tf_op jit(solution)/shard_map/adjoint/pallas_call | solution.py:306
  (5 shorter events, 0.0 us)
Async XLA Ops:
  18.7 66.2 %all-to-all-start = ((bf16[128,136,128]{2,1,0:T(8,128)(2,1)}), bf16[128,136,128]{2,1,0:T(8,128)(2,1)}, u32[]{:S(2)}, u32[]{:S(2)}) async-start(bf16[128,136,128]{2,1,0:T(8,128)(2,1)} %get-tuple-element.14), calls=%async_computation | async-start | bytes 8912896 | tf_op jit(solution)/shard_map/all_to_all | solution.py:398
  84.9 57.2 %all-to-all-start.1 = ((bf16[128,2,64,128]{3,2,1,0:T(8,128)(2,1)}), bf16[128,2,64,128]{3,2,1,0:T(8,128)(2,1)}, u32[]{:S(2)}, u32[]{:S(2)}) async-start(bf16[128,2,64,128]{3,2,1,0:T(8,128)(2,1)} %late.1), calls=%async_computation.1 | async-start | bytes 8388608 | tf_op jit(solution)/shard_map/all_to_all | solution.py:400
  142.1 65.0 %all-to-all-start.3 = ((bf16[128,2,64,128]{3,2,1,0:T(8,128)(2,1)}), bf16[128,2,64,128]{3,2,1,0:T(8,128)(2,1)}, u32[]{:S(2)}, u32[]{:S(2)}) async-start(bf16[128,2,64,128]{3,2,1,0:T(8,128)(2,1)} %bitcast.37), calls=%async_computation.3 | async-start | bytes 8388608 | tf_op jit(solution)/shard_map/all_to_all | solution.py:407
  174.3 24.8 %collective-permute-start = (f32[2,48,128]{2,1,0:T(8,128)S(1)}, f32[2,48,128]{2,1,0:T(8,128)S(1)}, u32[]{:S(2)}, u32[]{:S(2)}) collective-permute-start(f32[2,48,128]{2,1,0:T(8,128)S(1)} %bitcast.46), channel_id=1, source_target_pairs={{0,16},{16,32},{32,48},{48,64},{64,80},{80,96},{96,112},{1,17},{17... | collective-permute-start | bytes 147464 | tf_op jit(solution)/shard_map/ppermute | solution.py:332
  175.6 23.5 %collective-permute-start.1 = (f32[2,48,128]{2,1,0:T(8,128)S(1)}, f32[2,48,128]{2,1,0:T(8,128)S(1)}, u32[]{:S(2)}, u32[]{:S(2)}) collective-permute-start(f32[2,48,128]{2,1,0:T(8,128)S(1)} %bitcast.45), channel_id=1, source_target_pairs={{16,0},{32,16},{48,32},{64,48},{80,64},{96,80},{112,96},{17,1},{33... | collective-permute-start | bytes 147464 | tf_op jit(solution)/shard_map/ppermute | solution.py:335
  178.6 20.5 %copy-start = (f32[1536,128]{1,0:T(8,128)S(1)}, f32[1536,128]{1,0:T(8,128)}, u32[]{:S(2)}) copy-start(f32[1536,128]{1,0:T(8,128)} %get-tuple-element.18) | copy-start | bytes 2359300
  199.2 4.4 %collective-permute-start.2 = (f32[36,2,128]{2,1,0:T(2,128)S(1)}, f32[36,2,128]{2,1,0:T(2,128)S(1)}, u32[]{:S(2)}, u32[]{:S(2)}) collective-permute-start(f32[36,2,128]{2,1,0:T(2,128)S(1)} %get-tuple-element.32), channel_id=1, source_target_pairs={{0,1},{1,2},{2,3},{3,4},{4,5},{5,6},{6,7},{7,8},{8,9},{9,10},{10,1... | collective-permute-start | bytes 110600 | tf_op jit(solution)/shard_map/ppermute | solution.py:332
  202.3 4.7 %collective-permute-start.3 = (f32[36,2,128]{2,1,0:T(2,128)S(1)}, f32[36,2,128]{2,1,0:T(2,128)S(1)}, u32[]{:S(2)}, u32[]{:S(2)}) collective-permute-start(f32[36,2,128]{2,1,0:T(2,128)S(1)} %get-tuple-element.33), channel_id=1, source_target_pairs={{1,0},{2,1},{3,2},{4,3},{5,4},{6,5},{7,6},{8,7},{9,8},{10,9},{11,1... | collective-permute-start | bytes 110600 | tf_op jit(solution)/shard_map/ppermute | solution.py:335
  207.1 15.5 %copy-start.1 = (s32[1,128,2,128]{3,2,1,0:T(2,128)S(1)}, s32[1,128,2,128]{3,2,1,0:T(2,128)}, u32[]{:S(2)}) copy-start(s32[1,128,2,128]{3,2,1,0:T(2,128)} %param.8) | copy-start | bytes 393220
  207.1 66.5 %all-to-all-start.2 = ((bf16[128,2,64,128]{3,2,1,0:T(8,128)(2,1)}), bf16[128,2,64,128]{3,2,1,0:T(8,128)(2,1)}, u32[]{:S(2)}, u32[]{:S(2)}) async-start(bf16[128,2,64,128]{3,2,1,0:T(8,128)(2,1)} %bitcast.36), calls=%async_computation.2 | async-start | bytes 8388608 | tf_op jit(solution)/shard_map/all_to_all | solution.py:425

commit v3 on v2

--- a/solution.py
+++ b/solution.py
@@ -10,12 +10,12 @@
 CIL = 32
 CXL = 48
 LOW = 256
-GROUP = 8
+GROUP = 32
 BF = jnp.bfloat16
 F32 = jnp.float32
 
 
-def prep_kernel(blocks, traces, rev, cells, out, filt, mats):
+def prep_kernel(blocks, counts, traces, taps, cells, out, filt, mats, wide):
     surveys = mats.shape[0]
     samples = mats.shape[1]
     rows = traces.shape[0] // surveys
@@ -26,17 +26,19 @@
 
     @pl.when(step == 0)
     def _():
-        t_id = lax.broadcasted_iota(jnp.int32, (samples, samples), 0)
-        u_id = lax.broadcasted_iota(jnp.int32, (samples, samples), 1)
+        u_id = lax.broadcasted_iota(jnp.int32, (samples, samples), 0)
+        t_id = lax.broadcasted_iota(jnp.int32, (samples, samples), 1)
+        wide[...] = jnp.zeros_like(wide)
+        wide[:, : taps.shape[1]] = taps[...]
         for s in range(surveys):
-            base = jnp.broadcast_to(rev[s : s + 1, :], (samples, samples))
+            base = jnp.broadcast_to(wide[s : s + 1, :], (samples, samples))
             skew = pltpu.roll(base, 0, 1, stride=1, stride_axis=0)
             mat = jnp.where(u_id <= t_id, skew, 0.0).astype(BF)
             mats[s] = mat
             res = lax.dot_general(
                 mat,
                 traces[s * rows : (s + 1) * rows, :],
-                (((1,), (1,)), ((), ())),
+                (((0,), (1,)), ((), ())),
                 preferred_element_type=F32,
             ).astype(BF)
             for b in range(per):
@@ -44,15 +46,17 @@
 
     for k in range(tiles):
         for c in range(slots):
-            block = blocks[(step * tiles + k) * slots + c]
+            block = blocks[c * (blocks.shape[0] // slots) + step * tiles + k]
             out[k, c * part : (c + 1) * part, :] = filt[block, :part, :]
-        here = cells[k]
+        live = lax.broadcasted_iota(jnp.int32, (slots, samples), 0) < counts[step * tiles + k]
+        here = jnp.where(live, cells[k], -1)
         tags = [here & (LOW - 1), here >> 8, jnp.zeros((8 - 2 * slots, samples), jnp.int32)]
         out[k, slots * part :, :] = jnp.concatenate(tags, axis=0).astype(F32).astype(BF)
 
 
-def prep(traces, rev, blocks, cells, surveys):
-    tiles = 8
+def prep(traces, taps, blocks, counts, cells):
+    tiles = 32
+    surveys = taps.shape[0]
     devices, slots, samples = cells.shape
     nblk = traces.shape[0] // samples
     part = samples // 2
@@ -60,11 +64,11 @@
     return pl.pallas_call(
         prep_kernel,
         grid_spec=pltpu.PrefetchScalarGridSpec(
-            num_scalar_prefetch=1,
+            num_scalar_prefetch=2,
             grid=(devices // tiles,),
             in_specs=[
                 full(*traces.shape),
-                full(*rev.shape),
+                full(*taps.shape),
                 pl.BlockSpec((tiles, slots, samples), lambda i, *_: (i, 0, 0)),
             ],
             out_specs=[
@@ -72,6 +76,7 @@
                 full(nblk, samples, samples),
                 full(surveys, samples, samples),
             ],
+            scratch_shapes=[pltpu.VMEM((surveys, samples), F32)],
         ),
         out_shape=[
             jax.ShapeDtypeStruct((devices, slots * part + 8, samples), BF),
@@ -79,7 +84,7 @@
             jax.ShapeDtypeStruct((surveys, samples, samples), BF),
         ],
         name="prep",
-    )(blocks, traces, rev, cells)
+    )(blocks, counts, traces, taps, cells)
 
 
 def late_kernel(blocks, filt, out):
@@ -87,11 +92,11 @@
     step = pl.program_id(0)
     for k in range(tiles):
         for c in range(slots):
-            out[k, c] = filt[blocks[(step * tiles + k) * slots + c], part:, :]
+            out[k, c] = filt[blocks[c * (blocks.shape[0] // slots) + step * tiles + k], part:, :]
 
 
 def late(blocks, filt, devices, slots):
-    tiles = 8
+    tiles = 32
     nblk, samples, lanes = filt.shape
     part = samples // 2
     return pl.pallas_call(
@@ -112,8 +117,9 @@
 
 
 def low_hot(cells, lanes):
-    ids = lax.broadcasted_iota(jnp.int32, (LOW, lanes), 0)
-    return (ids == (cells & (LOW - 1))).astype(F32).astype(BF)
+    ids = lax.broadcasted_iota(jnp.int32, (LOW, lanes), 0).astype(F32).astype(BF)
+    low = jnp.broadcast_to((cells & (LOW - 1)).astype(F32).astype(BF), (LOW, lanes))
+    return jnp.where(ids == low, jnp.ones((), BF), jnp.zeros((), BF))
 
 
 def fill(cells, pick, samples, left, hot):
@@ -254,8 +260,8 @@
     )(cells, half)
 
 
-def subtract(first, blocks, block_rows, cells, back, filt, acc):
-    nblk, part = acc.shape[:2]
+def subtract(blocks, block_rows, cells, back, filt, acc):
+    nblk = acc.shape[0]
     tiles, slots = back.shape[:2]
     step = pl.program_id(0)
 
@@ -266,16 +272,16 @@
         pick = (ids == block_rows[...]).astype(F32).astype(BF)
         count = jnp.dot(pick, live, preferred_element_type=F32)
         for b in range(nblk):
-            acc[b] = filt[b, first : first + part, :].astype(F32) * count[b : b + 1, :]
+            acc[b] = filt[b].astype(F32) * count[b : b + 1, :]
 
     for k in range(tiles):
         for c in range(slots):
-            b = blocks[(step * tiles + k) * slots + c]
+            b = blocks[c * (blocks.shape[0] // slots) + step * tiles + k]
             acc[b] = acc[b] - back[k, c].astype(F32)
 
 
 def misfit_kernel(blocks, block_rows, cells, back, filt, out, acc):
-    subtract(0, blocks, block_rows, cells, back, filt, acc)
+    subtract(blocks, block_rows, cells, back, filt, acc)
 
     @pl.when(pl.program_id(0) == pl.num_programs(0) - 1)
     def _():
@@ -284,7 +290,7 @@
 
 def adjoint_kernel(blocks, block_rows, cells, back, filt, early, mats, out, acc):
     nblk, part, lanes = acc.shape
-    subtract(part, blocks, block_rows, cells, back, filt, acc)
+    subtract(blocks, block_rows, cells, back, filt, acc)
     per = nblk // mats.shape[0]
 
     @pl.when(pl.program_id(0) == pl.num_programs(0) - 1)
@@ -293,13 +299,13 @@
             out[b * lanes : (b + 1) * lanes, :] = lax.dot_general(
                 jnp.concatenate([early[b], acc[b].astype(BF)], axis=0),
                 mats[b // per],
-                (((0,), (0,)), ((), ())),
+                (((0,), (1,)), ((), ())),
                 preferred_element_type=F32,
             )
 
 
-def owner_call(kernel, blocks, cells, back, rest, out_shape, name):
-    tiles = 8
+def owner_call(kernel, which, blocks, block_rows, cells, back, rest, out_shape, name):
+    tiles = 16
     devices, slots, part, lanes = back.shape
     nblk = rest[0].shape[0]
     full = lambda *shape: pl.BlockSpec(shape, lambda i, *_: (0,) * len(shape))
@@ -313,7 +319,8 @@
                 full(*cells.shape),
                 pl.BlockSpec((tiles, slots, part, lanes), lambda i, *_: (i, 0, 0, 0)),
             ]
-            + [full(*x.shape) for x in rest],
+            + [pl.BlockSpec((nblk, part, lanes), lambda i, *_: (0, which, 0))]
+            + [full(*x.shape) for x in rest[1:]],
             out_specs=full(*out_shape.shape),
             scratch_shapes=[pltpu.VMEM((nblk, part, lanes), F32)],
         ),
@@ -322,7 +329,7 @@
             flops=0, bytes_accessed=back.size * 2 + rest[0].size * 4, transcendentals=0
         ),
         name=name,
-    )(blocks, blocks[None, :], cells, back, *rest)
+    )(blocks, block_rows, cells, back, *rest)
 
 
 def edges(block, axis, dim, width):
@@ -380,7 +387,6 @@
     rows, samples = traces.shape
     slots = slot_block.shape[2]
     lanes = slot_cells.shape[3]
-    surveys, taps = filter_taps.shape
     cell_count = CIL * CXL
     part = samples // 2
     flat = (devices * slots, part, lanes)
@@ -389,12 +395,13 @@
     swap = functools.partial(
         lax.all_to_all, axis_name=("il", "xl"), split_axis=0, concat_axis=0, tiled=True
     )
-    wide = jnp.pad(filter_taps, ((0, 0), (0, samples - taps)))
-    rev = jnp.roll(wide[:, ::-1], 1, axis=1)
-    blocks = slot_block[0].reshape(-1)
+    blocks = slot_block[0].T.reshape(-1)
+    block_rows = slot_block[0].reshape(1, -1)
     slot_live = jnp.arange(slots, dtype=jnp.int32)[None, :] < pair_count[0][:, None]
     out_cells = jnp.where(slot_live[:, :, None], slot_cells[0], -1)
-    out_early, filt, mats = prep(traces, rev, blocks, out_cells, surveys)
+    out_early, filt, mats = prep(
+        traces, filter_taps, blocks, pair_count.reshape(-1), slot_cells[0]
+    )
     in_early = swap(out_early)
     out_late = late(blocks, filt, devices, slots)
     in_late = swap(out_late)
@@ -427,7 +434,9 @@
     mine = out_cells.reshape(-1, lanes)
     early = owner_call(
         misfit_kernel,
+        0,
         blocks,
+        block_rows,
         mine,
         back_early,
         (filt,),
@@ -436,7 +445,9 @@
     )
     adjoint_traces = owner_call(
         adjoint_kernel,
+        1,
         blocks,
+        block_rows,
         mine,
         back_late,
         (filt, early, mats),

time: 292 us -> 267 us (0.914)
  the two profiles are of different devices: /device:TPU:7 before, /device:TPU:62 now
where the time goes in v3:
time: 267 us; the launch traced here: 262 us
  waiting for transfers between devices  117 us (44%)
  Pallas kernels  83.4 us (31%)
  starting transfers between devices  47.1 us (18%)
  other arithmetic  12.1 us (5%)
    all_to_all x1, waiting for transfers between devices, local(): in_early = swap(out_early)  47.2 us
    pallas_call x2, Pallas kernels, binned(): pl.pallas_call(kernel, grid=(slots // GROUP,), in_specs=[pl.BlockSpec((GR...  31.7 us
    all_to_all x1, waiting for transfers between devices, local(): back_late = swap(answer_late.reshape(boxed))  30 us
    pallas_call x2, Pallas kernels, read(): pl.pallas_call(read_kernel, grid=(slots // GROUP,), in_specs=[pl.BlockSpe...  21.5 us
    all_to_all x1, waiting for transfers between devices, local(): in_late = swap(out_late)  21 us
    pallas_call x2, Pallas kernels, owner_call(): pl.pallas_call(kernel, grid_spec=pltpu.PrefetchScalarGridSpec(num_scalar_...  18.1 us
    ppermute x2, waiting for transfers between devices, edges(): lax.ppermute(lax.slice_in_dim(block, block.shape[dim] - width, None, axis...  12.9 us
    all_to_all x1, starting transfers between devices, local(): in_early = swap(out_early)  10.5 us
  transfers between devices with their start and end apart: 8, of which 5 were waited for; matrix products, arithmetic and copies ran while one was open for 5% of the time, Pallas kernels for 25%

profile of v3, /device:TPU:62, one launch (start us, length us, event | category | flops | bytes accessed | tf_op | source)
XLA Modules:
  0.0 262.4 jit_solution(15794432098321450782)
XLA Ops:
  0.6 7.3 %prep.1 = (bf16[128,136,128]{2,1,0:T(8,128)(2,1)}, bf16[60,128,128]{2,1,0:T(8,128)(2,1)}, bf16[12,128,128]{2,1,0:T(8,128)(2,1)}) custom-call(s32[256]{0:T(256)} %bitcast.51, s32[128]{0:T(128)} %bitcast.55, bf16[7680,128]{1,0:T(8,128)(2,1)} %traces.1, f32[12,64]{1,0:T(8,128)} %taps.1, s32[128,2,128]{2,1,0:T(2,128)} %bitcast.43), custom_call_target="tpu_custom_call" | custom-call | tf_op jit(solution)/shard_map/prep/pallas_call | solution.py:64
  7.9 10.5 %all-to-all-start = ((bf16[128,136,128]{2,1,0:T(8,128)(2,1)}), bf16[128,136,128]{2,1,0:T(8,128)(2,1)}, u32[]{:S(2)}, u32[]{:S(2)}) async-start(bf16[128,136,128]{2,1,0:T(8,128)(2,1)} %get-tuple-element.14), calls=%async_computation | async-start | bytes 8912896 | tf_op jit(solution)/shard_map/all_to_all | solution.py:405
  18.4 4.8 %late.1 = bf16[128,2,64,128]{3,2,1,0:T(8,128)(2,1)} custom-call(s32[256]{0:T(256)} %bitcast.52, bf16[60,128,128]{2,1,0:T(8,128)(2,1)} %get-tuple-element.15.filt), custom_call_target="tpu_custom_call" | custom-call | bytes 6160384 | tf_op jit(solution)/shard_map/late/pallas_call | solution.py:102
  23.2 47.2 %all-to-all-done.data = bf16[128,136,128]{2,1,0:T(8,128)(2,1)} async-done(((bf16[128,136,128]{2,1,0:T(8,128)(2,1)}), bf16[128,136,128]{2,1,0:T(8,128)(2,1)}, u32[]{:S(2)}, u32[]{:S(2)}) %all-to-all-start) | async-done | bytes 4456480 | tf_op jit(solution)/shard_map/all_to_all | solution.py:405
  70.3 8.3 %all-to-all-start.1 = ((bf16[128,2,64,128]{3,2,1,0:T(8,128)(2,1)}), bf16[128,2,64,128]{3,2,1,0:T(8,128)(2,1)}, u32[]{:S(2)}, u32[]{:S(2)}) async-start(bf16[128,2,64,128]{3,2,1,0:T(8,128)(2,1)} %late.1), calls=%async_computation.1 | async-start | bytes 8388608 | tf_op jit(solution)/shard_map/all_to_all | solution.py:407
  78.7 1.0 slice_convert_fusion
  79.7 0.8 slice_add_fusion.48
  80.4 15.7 %bin_early.1 = (bf16[384,256]{1,0:T(8,128)(2,1)}, f32[384,256]{1,0:T(8,128)}) custom-call(s32[256,128]{1,0:T(8,128)} %bitcast.45, bf16[128,136,128]{2,1,0:T(8,128)(2,1)} %all-to-all-done.data), custom_call_target="tpu_custom_call" | custom-call | flops 6710886400 | bytes 4456448 | tf_op jit(solution)/shard_map/bin_early/pallas_call | solution.py:199
  96.1 10.7 %read_early.1 = bf16[256,64,128]{2,1,0:T(8,128)(2,1)} custom-call(s32[256,128]{1,0:T(8,128)} %bitcast.46, bf16[384,256]{1,0:T(8,128)(2,1)} %get-tuple-element.24.half), custom_call_target="tpu_custom_call" | custom-call | flops 6442450944 | bytes 4194304 | tf_op jit(solution)/shard_map/read_early/pallas_call | solution.py:244
  106.8 21.0 %all-to-all-done.1 = bf16[128,2,64,128]{3,2,1,0:T(8,128)(2,1)} async-done(((bf16[128,2,64,128]{3,2,1,0:T(8,128)(2,1)}), bf16[128,2,64,128]{3,2,1,0:T(8,128)(2,1)}, u32[]{:S(2)}, u32[]{:S(2)}) %all-to-all-start.1) | async-done | bytes 4194336 | tf_op jit(solution)/shard_map/all_to_all | solution.py:407
  127.8 8.0 %all-to-all-start.3 = ((bf16[128,2,64,128]{3,2,1,0:T(8,128)(2,1)}), bf16[128,2,64,128]{3,2,1,0:T(8,128)(2,1)}, u32[]{:S(2)}, u32[]{:S(2)}) async-start(bf16[128,2,64,128]{3,2,1,0:T(8,128)(2,1)} %bitcast.40), calls=%async_computation.3 | async-start | bytes 8388608 | tf_op jit(solution)/shard_map/all_to_all | solution.py:414
  135.8 16.1 %bin_late.1 = (bf16[384,256]{1,0:T(8,128)(2,1)}, f32[1536,128]{1,0:T(8,128)}) custom-call(s32[256,128]{1,0:T(8,128)} %bitcast.47, bf16[256,64,128]{2,1,0:T(8,128)(2,1)} %bitcast.8.data, f32[384,256]{1,0:T(8,128)} %get-tuple-element.16.value), custom_call_target="tpu_custom_call" | custom-call | flops 6710886400 | bytes 4194304 | tf_op jit(solution)/shard_map/bin_late/pallas_call | solution.py:199
  151.8 0.8 fusion.20
  152.7 2.0 collective-permute-start
  154.7 3.5 %collective-permute-start.1 = (f32[2,48,128]{2,1,0:T(8,128)S(1)}, f32[2,48,128]{2,1,0:T(8,128)S(1)}, u32[]{:S(2)}, u32[]{:S(2)}) collective-permute-start(f32[2,48,128]{2,1,0:T(8,128)S(1)} %bitcast.49), channel_id=1, source_target_pairs={{16,0},{32,16},{48,32},{64,48},{80,64},{96,80},{112,96},{17,1},{33... | collective-permute-start | bytes 147464 | tf_op jit(solution)/shard_map/ppermute | solution.py:342
  158.2 0.0 copy-start
  158.3 10.8 %read_late.1 = bf16[256,64,128]{2,1,0:T(8,128)(2,1)} custom-call(s32[256,128]{1,0:T(8,128)} %bitcast.48, bf16[384,256]{1,0:T(8,128)(2,1)} %get-tuple-element.17.half), custom_call_target="tpu_custom_call" | custom-call | flops 6442450944 | bytes 4194304 | tf_op jit(solution)/shard_map/read_late/pallas_call | solution.py:244
  169.0 12.9 %collective-permute-done = f32[2,48,128]{2,1,0:T(8,128)S(1)} collective-permute-done((f32[2,48,128]{2,1,0:T(8,128)S(1)}, f32[2,48,128]{2,1,0:T(8,128)S(1)}, u32[]{:S(2)}, u32[]{:S(2)}) %collective-permute-start) | collective-permute-done | bytes 49184 | tf_op jit(solution)/shard_map/ppermute | solution.py:339
  182.0 0.0 collective-permute-done.1
  182.0 0.0 copy-done
  182.0 4.4 %collective-permute-start.2 = (f32[36,2,128]{2,1,0:T(2,128)S(1)}, f32[36,2,128]{2,1,0:T(2,128)S(1)}, u32[]{:S(2)}, u32[]{:S(2)}) collective-permute-start(f32[36,2,128]{2,1,0:T(2,128)S(1)} %get-tuple-element.32), channel_id=1, source_target_pairs={{0,1},{1,2},{2,3},{3,4},{4,5},{5,6},{6,7},{7,8},{8,9},{9,10},{10,1... | collective-permute-start | bytes 110600 | tf_op jit(solution)/shard_map/ppermute | solution.py:339
  186.4 0.0 copy-start.2
  186.4 1.9 collective-permute-start.3
  188.3 0.0 collective-permute-done.2
  188.3 6.0 %collective-permute-done.3 = f32[36,2,128]{2,1,0:T(2,128)S(1)} collective-permute-done((f32[36,2,128]{2,1,0:T(2,128)S(1)}, f32[36,2,128]{2,1,0:T(2,128)S(1)}, u32[]{:S(2)}, u32[]{:S(2)}) %collective-permute-start.3) | collective-permute-done | bytes 36896 | tf_op jit(solution)/shard_map/ppermute | solution.py:342
  194.4 0.1 pad_maximum_fusion
  194.5 0.0 copy-start.3
  194.5 0.0 copy-start.1
  194.5 0.0 all-to-all-done.3.back
  194.5 8.5 %all-to-all-start.2 = ((bf16[128,2,64,128]{3,2,1,0:T(8,128)(2,1)}), bf16[128,2,64,128]{3,2,1,0:T(8,128)(2,1)}, u32[]{:S(2)}, u32[]{:S(2)}) async-start(bf16[128,2,64,128]{3,2,1,0:T(8,128)(2,1)} %bitcast.39), calls=%async_computation.2 | async-start | bytes 8388608 | tf_op jit(solution)/shard_map/all_to_all | solution.py:432
  203.0 0.0 copy-done.2
  203.0 0.1 copy.8
  203.1 0.0 copy-done.3
  203.2 0.1 iota_compare_fusion
  203.2 0.1 lt.47
  203.4 0.7 reshape_squeeze.3.block_rows
  204.1 0.1 broadcast_multiply_fusion
  204.2 0.7 broadcast_select_fusion.cells
  204.9 2.0 multiply_multiply_fusion
  206.9 1.2 fusion.19
  208.2 1.2 fusion.16
  209.4 1.2 fusion.13
  210.6 1.2 fusion.10
  211.8 1.2 fusion.7
  213.0 1.2 fusion.4
  214.3 7.8 %misfit.1.early = bf16[60,64,128]{2,1,0:T(8,128)(2,1)} custom-call(s32[256]{0:T(256)} %bitcast.53, s32[1,256]{1,0:T(1,128)} %reshape_squeeze.3.block_rows, s32[256,128]{1,0:T(8,128)} %broadcast_select_fusion.cells, bf16[128,2,64,128]{3,2,1,0:T(8,128)(2,1)} %all-to-all-done.3.back, bf16[60,128,128]{2,1,0:T(8,128)(2,1)} %get-tuple-element.15.filt), custom_call_target="tpu_custom_call" | custom-call | bytes 8126464 | tf_op jit(solution)/shard_map/misfit/pallas_call | solution.py:312
  222.0 30.0 %all-to-all-done.2.back = bf16[128,2,64,128]{3,2,1,0:T(8,128)(2,1)} async-done(((bf16[128,2,64,128]{3,2,1,0:T(8,128)(2,1)}), bf16[128,2,64,128]{3,2,1,0:T(8,128)(2,1)}, u32[]{:S(2)}, u32[]{:S(2)}) %all-to-all-start.2) | async-done | bytes 4194336 | tf_op jit(solution)/shard_map/all_to_all | solution.py:432
  252.1 10.3 %adjoint.1 = f32[7680,128]{1,0:T(8,128)} custom-call(s32[256]{0:T(256)} %bitcast.54, s32[1,256]{1,0:T(1,128)} %reshape_squeeze.3.block_rows, s32[256,128]{1,0:T(8,128)} %broadcast_select_fusion.cells, bf16[128,2,64,128]{3,2,1,0:T(8,128)(2,1)} %all-to-all-done.2.back, bf16[60,128,128]{2,1,0:T(8,128)(2,1)} %get-tuple-element.15.filt, ...), custom_call_target="tpu_custom_call" | custom-call | bytes 8126464 | tf_op jit(solution)/shard_map/adjoint/pallas_call | solution.py:312
  (4 shorter events, 0.0 us)
Async XLA Ops:
  7.9 62.4 %all-to-all-start = ((bf16[128,136,128]{2,1,0:T(8,128)(2,1)}), bf16[128,136,128]{2,1,0:T(8,128)(2,1)}, u32[]{:S(2)}, u32[]{:S(2)}) async-start(bf16[128,136,128]{2,1,0:T(8,128)(2,1)} %get-tuple-element.14), calls=%async_computation | async-start | bytes 8912896 | tf_op jit(solution)/shard_map/all_to_all | solution.py:405
  70.3 57.4 %all-to-all-start.1 = ((bf16[128,2,64,128]{3,2,1,0:T(8,128)(2,1)}), bf16[128,2,64,128]{3,2,1,0:T(8,128)(2,1)}, u32[]{:S(2)}, u32[]{:S(2)}) async-start(bf16[128,2,64,128]{3,2,1,0:T(8,128)(2,1)} %late.1), calls=%async_computation.1 | async-start | bytes 8388608 | tf_op jit(solution)/shard_map/all_to_all | solution.py:407
  127.8 66.7 %all-to-all-start.3 = ((bf16[128,2,64,128]{3,2,1,0:T(8,128)(2,1)}), bf16[128,2,64,128]{3,2,1,0:T(8,128)(2,1)}, u32[]{:S(2)}, u32[]{:S(2)}) async-start(bf16[128,2,64,128]{3,2,1,0:T(8,128)(2,1)} %bitcast.40), calls=%async_computation.3 | async-start | bytes 8388608 | tf_op jit(solution)/shard_map/all_to_all | solution.py:414
  152.7 29.3 %collective-permute-start = (f32[2,48,128]{2,1,0:T(8,128)S(1)}, f32[2,48,128]{2,1,0:T(8,128)S(1)}, u32[]{:S(2)}, u32[]{:S(2)}) collective-permute-start(f32[2,48,128]{2,1,0:T(8,128)S(1)} %bitcast.50), channel_id=1, source_target_pairs={{0,16},{16,32},{32,48},{48,64},{64,80},{80,96},{96,112},{1,17},{17... | collective-permute-start | bytes 147464 | tf_op jit(solution)/shard_map/ppermute | solution.py:339
  154.7 27.2 %collective-permute-start.1 = (f32[2,48,128]{2,1,0:T(8,128)S(1)}, f32[2,48,128]{2,1,0:T(8,128)S(1)}, u32[]{:S(2)}, u32[]{:S(2)}) collective-permute-start(f32[2,48,128]{2,1,0:T(8,128)S(1)} %bitcast.49), channel_id=1, source_target_pairs={{16,0},{32,16},{48,32},{64,48},{80,64},{96,80},{112,96},{17,1},{33... | collective-permute-start | bytes 147464 | tf_op jit(solution)/shard_map/ppermute | solution.py:342
  158.2 23.7 %copy-start = (f32[1536,128]{1,0:T(8,128)S(1)}, f32[1536,128]{1,0:T(8,128)}, u32[]{:S(2)}) copy-start(f32[1536,128]{1,0:T(8,128)} %get-tuple-element.18) | copy-start | bytes 2359300
  182.0 6.3 %collective-permute-start.2 = (f32[36,2,128]{2,1,0:T(2,128)S(1)}, f32[36,2,128]{2,1,0:T(2,128)S(1)}, u32[]{:S(2)}, u32[]{:S(2)}) collective-permute-start(f32[36,2,128]{2,1,0:T(2,128)S(1)} %get-tuple-element.32), channel_id=1, source_target_pairs={{0,1},{1,2},{2,3},{3,4},{4,5},{5,6},{6,7},{7,8},{8,9},{9,10},{10,1... | collective-permute-start | bytes 110600 | tf_op jit(solution)/shard_map/ppermute | solution.py:339
  186.4 16.6 %copy-start.2 = (s32[1,128,2]{1,2,0:T(2,128)S(1)}, s32[1,128,2]{1,2,0:T(2,128)}, u32[]{:S(2)}) copy-start(s32[1,128,2]{1,2,0:T(2,128)} %param.7) | copy-start | bytes 3076
  186.4 8.0 %collective-permute-start.3 = (f32[36,2,128]{2,1,0:T(2,128)S(1)}, f32[36,2,128]{2,1,0:T(2,128)S(1)}, u32[]{:S(2)}, u32[]{:S(2)}) collective-permute-start(f32[36,2,128]{2,1,0:T(2,128)S(1)} %get-tuple-element.33), channel_id=1, source_target_pairs={{1,0},{2,1},{3,2},{4,3},{5,4},{6,5},{7,6},{8,7},{9,8},{10,9},{11,1... | collective-permute-start | bytes 110600 | tf_op jit(solution)/shard_map/ppermute | solution.py:342
  194.5 8.7 %copy-start.3 = (s32[1,128]{1,0:T(1,128)S(1)}, s32[1,128]{1,0:T(1,128)}, u32[]{:S(2)}) copy-start(s32[1,128]{1,0:T(1,128)} %param.9) | copy-start | bytes 1540
  194.5 9.7 %copy-start.1 = (s32[1,128,2,128]{3,2,1,0:T(2,128)S(1)}, s32[1,128,2,128]{3,2,1,0:T(2,128)}, u32[]{:S(2)}) copy-start(s32[1,128,2,128]{3,2,1,0:T(2,128)} %param.8) | copy-start | bytes 393220
  194.5 57.6 %all-to-all-start.2 = ((bf16[128,2,64,128]{3,2,1,0:T(8,128)(2,1)}), bf16[128,2,64,128]{3,2,1,0:T(8,128)(2,1)}, u32[]{:S(2)}, u32[]{:S(2)}) async-start(bf16[128,2,64,128]{3,2,1,0:T(8,128)(2,1)} %bitcast.39), calls=%async_computation.2 | async-start | bytes 8388608 | tf_op jit(solution)/shard_map/all_to_all | solution.py:432

commit v4 on v3

--- a/solution.py
+++ b/solution.py
@@ -15,7 +15,9 @@
 F32 = jnp.float32
 
 
-def prep_kernel(blocks, counts, traces, taps, cells, out, filt, mats, wide):
+def prep_kernel(
+    blocks, counts, traces, taps, cells, out, filt_out, mats_out, wide, filt, mats, sems
+):
     surveys = mats.shape[0]
     samples = mats.shape[1]
     rows = traces.shape[0] // surveys
@@ -23,6 +25,10 @@
     tiles, slots = cells.shape[:2]
     part = samples // 2
     step = pl.program_id(0)
+    leaving = (
+        pltpu.make_async_copy(filt, filt_out, sems.at[0]),
+        pltpu.make_async_copy(mats, mats_out, sems.at[1]),
+    )
 
     @pl.when(step == 0)
     def _():
@@ -43,6 +49,8 @@
             ).astype(BF)
             for b in range(per):
                 filt[s * per + b] = res[:, b * samples : (b + 1) * samples]
+        for copy in leaving:
+            copy.start()
 
     for k in range(tiles):
         for c in range(slots):
@@ -52,6 +60,11 @@
         here = jnp.where(live, cells[k], -1)
         tags = [here & (LOW - 1), here >> 8, jnp.zeros((8 - 2 * slots, samples), jnp.int32)]
         out[k, slots * part :, :] = jnp.concatenate(tags, axis=0).astype(F32).astype(BF)
+
+    @pl.when(step == pl.num_programs(0) - 1)
+    def _():
+        for copy in leaving:
+            copy.wait()
 
 
 def prep(traces, taps, blocks, counts, cells):
@@ -73,10 +86,15 @@
             ],
             out_specs=[
                 pl.BlockSpec((tiles, slots * part + 8, samples), lambda i, *_: (i, 0, 0)),
-                full(nblk, samples, samples),
-                full(surveys, samples, samples),
+                pl.BlockSpec(memory_space=pl.ANY),
+                pl.BlockSpec(memory_space=pl.ANY),
             ],
-            scratch_shapes=[pltpu.VMEM((surveys, samples), F32)],
+            scratch_shapes=[
+                pltpu.VMEM((surveys, samples), F32),
+                pltpu.VMEM((nblk, samples, samples), BF),
+                pltpu.VMEM((surveys, samples, samples), BF),
+                pltpu.SemaphoreType.DMA((2,)),
+            ],
         ),
         out_shape=[
             jax.ShapeDtypeStruct((devices, slots * part + 8, samples), BF),
@@ -288,23 +306,32 @@
         out[...] = acc[...].astype(BF)
 
 
-def adjoint_kernel(blocks, block_rows, cells, back, filt, early, mats, out, acc):
+def adjoint_kernel(blocks, block_rows, cells, back, filt, early, mats, out, acc, held, sems):
     nblk, part, lanes = acc.shape
     subtract(blocks, block_rows, cells, back, filt, acc)
     per = nblk // mats.shape[0]
+    piece = nblk // sems.shape[0]
+
+    def leaving(k):
+        at = pl.ds(k * piece * lanes, piece * lanes)
+        return pltpu.make_async_copy(held.at[at], out.at[at], sems.at[k])
 
     @pl.when(pl.program_id(0) == pl.num_programs(0) - 1)
     def _():
         for b in range(nblk):
-            out[b * lanes : (b + 1) * lanes, :] = lax.dot_general(
+            held[b * lanes : (b + 1) * lanes, :] = lax.dot_general(
                 jnp.concatenate([early[b], acc[b].astype(BF)], axis=0),
                 mats[b // per],
                 (((0,), (1,)), ((), ())),
                 preferred_element_type=F32,
             )
-
-
-def owner_call(kernel, which, blocks, block_rows, cells, back, rest, out_shape, name):
+            if (b + 1) % piece == 0:
+                leaving(b // piece).start()
+        for k in range(nblk // piece):
+            leaving(k).wait()
+
+
+def owner_call(kernel, which, blocks, block_rows, cells, back, rest, out_shape, name, extra=()):
     tiles = 16
     devices, slots, part, lanes = back.shape
     nblk = rest[0].shape[0]
@@ -321,8 +348,8 @@
             ]
             + [pl.BlockSpec((nblk, part, lanes), lambda i, *_: (0, which, 0))]
             + [full(*x.shape) for x in rest[1:]],
-            out_specs=full(*out_shape.shape),
-            scratch_shapes=[pltpu.VMEM((nblk, part, lanes), F32)],
+            out_specs=pl.BlockSpec(memory_space=pl.ANY) if extra else full(*out_shape.shape),
+            scratch_shapes=[pltpu.VMEM((nblk, part, lanes), F32), *extra],
         ),
         out_shape=out_shape,
         cost_estimate=pl.CostEstimate(
@@ -453,6 +480,7 @@
         (filt, early, mats),
         jax.ShapeDtypeStruct((rows, samples), F32),
         "adjoint",
+        (pltpu.VMEM((rows, samples), F32), pltpu.SemaphoreType.DMA((6,))),
     )
     return (structure_tensor, adjoint_traces)
 

time: 267 us -> 266 us (level)
  no operation moved by 1% of the time
where the time goes in v4:
time: 266 us; the launch traced here: 261 us
  waiting for transfers between devices  117 us (44%)
  Pallas kernels  82.3 us (31%)
  starting transfers between devices  47.2 us (18%)
  other arithmetic  12.1 us (5%)
    all_to_all x1, waiting for transfers between devices, local(): in_early = swap(out_early)  47.2 us
    pallas_call x2, Pallas kernels, binned(): pl.pallas_call(kernel, grid=(slots // GROUP,), in_specs=[pl.BlockSpec((GR...  31.7 us
    all_to_all x1, waiting for transfers between devices, local(): back_late = swap(answer_late.reshape(boxed))  30 us
    pallas_call x2, Pallas kernels, read(): pl.pallas_call(read_kernel, grid=(slots // GROUP,), in_specs=[pl.BlockSpe...  21.5 us
    all_to_all x1, waiting for transfers between devices, local(): in_late = swap(out_late)  21 us
    pallas_call x2, Pallas kernels, owner_call(): pl.pallas_call(kernel, grid_spec=pltpu.PrefetchScalarGridSpec(num_scalar_...  17.1 us
    ppermute x2, waiting for transfers between devices, edges(): lax.ppermute(lax.slice_in_dim(block, block.shape[dim] - width, None, axis...  12.9 us
    all_to_all x1, starting transfers between devices, local(): in_early = swap(out_early)  10.5 us
  transfers between devices with their start and end apart: 8, of which 5 were waited for; matrix products, arithmetic and copies ran while one was open for 5% of the time, Pallas kernels for 25%

profile of v4, /device:TPU:62, one launch (start us, length us, event | category | flops | bytes accessed | tf_op | source)
XLA Modules:
  0.0 261.5 jit_solution(9564985649704029335)
XLA Ops:
  0.6 7.2 %prep.1 = (bf16[128,136,128]{2,1,0:T(8,128)(2,1)}, bf16[60,128,128]{2,1,0:T(8,128)(2,1)}, bf16[12,128,128]{2,1,0:T(8,128)(2,1)}) custom-call(s32[256]{0:T(256)} %bitcast.51, s32[128]{0:T(128)} %bitcast.55, bf16[7680,128]{1,0:T(8,128)(2,1)} %traces.1, f32[12,64]{1,0:T(8,128)} %taps.1, s32[128,2,128]{2,1,0:T(2,128)} %bitcast.43), custom_call_target="tpu_custom_call" | custom-call | tf_op jit(solution)/shard_map/prep/pallas_call | solution.py:77
  7.9 10.5 %all-to-all-start = ((bf16[128,136,128]{2,1,0:T(8,128)(2,1)}), bf16[128,136,128]{2,1,0:T(8,128)(2,1)}, u32[]{:S(2)}, u32[]{:S(2)}) async-start(bf16[128,136,128]{2,1,0:T(8,128)(2,1)} %get-tuple-element.14), calls=%async_computation | async-start | bytes 8912896 | tf_op jit(solution)/shard_map/all_to_all | solution.py:432
  18.3 4.8 %late.1 = bf16[128,2,64,128]{3,2,1,0:T(8,128)(2,1)} custom-call(s32[256]{0:T(256)} %bitcast.52, bf16[60,128,128]{2,1,0:T(8,128)(2,1)} %get-tuple-element.15.filt), custom_call_target="tpu_custom_call" | custom-call | bytes 6160384 | tf_op jit(solution)/shard_map/late/pallas_call | solution.py:120
  23.1 47.2 %all-to-all-done.data = bf16[128,136,128]{2,1,0:T(8,128)(2,1)} async-done(((bf16[128,136,128]{2,1,0:T(8,128)(2,1)}), bf16[128,136,128]{2,1,0:T(8,128)(2,1)}, u32[]{:S(2)}, u32[]{:S(2)}) %all-to-all-start) | async-done | bytes 4456480 | tf_op jit(solution)/shard_map/all_to_all | solution.py:432
  70.3 8.3 %all-to-all-start.1 = ((bf16[128,2,64,128]{3,2,1,0:T(8,128)(2,1)}), bf16[128,2,64,128]{3,2,1,0:T(8,128)(2,1)}, u32[]{:S(2)}, u32[]{:S(2)}) async-start(bf16[128,2,64,128]{3,2,1,0:T(8,128)(2,1)} %late.1), calls=%async_computation.1 | async-start | bytes 8388608 | tf_op jit(solution)/shard_map/all_to_all | solution.py:434
  78.6 1.0 slice_convert_fusion
  79.6 0.8 slice_add_fusion.48
  80.4 15.7 %bin_early.1 = (bf16[384,256]{1,0:T(8,128)(2,1)}, f32[384,256]{1,0:T(8,128)}) custom-call(s32[256,128]{1,0:T(8,128)} %bitcast.45, bf16[128,136,128]{2,1,0:T(8,128)(2,1)} %all-to-all-done.data), custom_call_target="tpu_custom_call" | custom-call | flops 6710886400 | bytes 4456448 | tf_op jit(solution)/shard_map/bin_early/pallas_call | solution.py:217
  96.0 10.7 %read_early.1 = bf16[256,64,128]{2,1,0:T(8,128)(2,1)} custom-call(s32[256,128]{1,0:T(8,128)} %bitcast.46, bf16[384,256]{1,0:T(8,128)(2,1)} %get-tuple-element.24.half), custom_call_target="tpu_custom_call" | custom-call | flops 6442450944 | bytes 4194304 | tf_op jit(solution)/shard_map/read_early/pallas_call | solution.py:262
  106.7 21.0 %all-to-all-done.1 = bf16[128,2,64,128]{3,2,1,0:T(8,128)(2,1)} async-done(((bf16[128,2,64,128]{3,2,1,0:T(8,128)(2,1)}), bf16[128,2,64,128]{3,2,1,0:T(8,128)(2,1)}, u32[]{:S(2)}, u32[]{:S(2)}) %all-to-all-start.1) | async-done | bytes 4194336 | tf_op jit(solution)/shard_map/all_to_all | solution.py:434
  127.7 8.0 %all-to-all-start.3 = ((bf16[128,2,64,128]{3,2,1,0:T(8,128)(2,1)}), bf16[128,2,64,128]{3,2,1,0:T(8,128)(2,1)}, u32[]{:S(2)}, u32[]{:S(2)}) async-start(bf16[128,2,64,128]{3,2,1,0:T(8,128)(2,1)} %bitcast.40), calls=%async_computation.3 | async-start | bytes 8388608 | tf_op jit(solution)/shard_map/all_to_all | solution.py:441
  135.7 16.1 %bin_late.1 = (bf16[384,256]{1,0:T(8,128)(2,1)}, f32[1536,128]{1,0:T(8,128)}) custom-call(s32[256,128]{1,0:T(8,128)} %bitcast.47, bf16[256,64,128]{2,1,0:T(8,128)(2,1)} %bitcast.8.data, f32[384,256]{1,0:T(8,128)} %get-tuple-element.16.value), custom_call_target="tpu_custom_call" | custom-call | flops 6710886400 | bytes 4194304 | tf_op jit(solution)/shard_map/bin_late/pallas_call | solution.py:217
  151.8 0.8 fusion.20
  152.6 2.0 collective-permute-start
  154.7 3.5 %collective-permute-start.1 = (f32[2,48,128]{2,1,0:T(8,128)S(1)}, f32[2,48,128]{2,1,0:T(8,128)S(1)}, u32[]{:S(2)}, u32[]{:S(2)}) collective-permute-start(f32[2,48,128]{2,1,0:T(8,128)S(1)} %bitcast.49), channel_id=1, source_target_pairs={{16,0},{32,16},{48,32},{64,48},{80,64},{96,80},{112,96},{17,1},{33... | collective-permute-start | bytes 147464 | tf_op jit(solution)/shard_map/ppermute | solution.py:369
  158.2 0.0 copy-start
  158.2 10.8 %read_late.1 = bf16[256,64,128]{2,1,0:T(8,128)(2,1)} custom-call(s32[256,128]{1,0:T(8,128)} %bitcast.48, bf16[384,256]{1,0:T(8,128)(2,1)} %get-tuple-element.17.half), custom_call_target="tpu_custom_call" | custom-call | flops 6442450944 | bytes 4194304 | tf_op jit(solution)/shard_map/read_late/pallas_call | solution.py:262
  169.0 12.9 %collective-permute-done = f32[2,48,128]{2,1,0:T(8,128)S(1)} collective-permute-done((f32[2,48,128]{2,1,0:T(8,128)S(1)}, f32[2,48,128]{2,1,0:T(8,128)S(1)}, u32[]{:S(2)}, u32[]{:S(2)}) %collective-permute-start) | collective-permute-done | bytes 49184 | tf_op jit(solution)/shard_map/ppermute | solution.py:366
  181.9 0.0 collective-permute-done.1
  181.9 0.0 copy-done
  181.9 4.4 %collective-permute-start.2 = (f32[36,2,128]{2,1,0:T(2,128)S(1)}, f32[36,2,128]{2,1,0:T(2,128)S(1)}, u32[]{:S(2)}, u32[]{:S(2)}) collective-permute-start(f32[36,2,128]{2,1,0:T(2,128)S(1)} %get-tuple-element.32), channel_id=1, source_target_pairs={{0,1},{1,2},{2,3},{3,4},{4,5},{5,6},{6,7},{7,8},{8,9},{9,10},{10,1... | collective-permute-start | bytes 110600 | tf_op jit(solution)/shard_map/ppermute | solution.py:366
  186.3 0.0 copy-start.2
  186.3 1.9 collective-permute-start.3
  188.3 0.0 collective-permute-done.2
  188.3 6.0 %collective-permute-done.3 = f32[36,2,128]{2,1,0:T(2,128)S(1)} collective-permute-done((f32[36,2,128]{2,1,0:T(2,128)S(1)}, f32[36,2,128]{2,1,0:T(2,128)S(1)}, u32[]{:S(2)}, u32[]{:S(2)}) %collective-permute-start.3) | collective-permute-done | bytes 36896 | tf_op jit(solution)/shard_map/ppermute | solution.py:369
  194.3 0.1 pad_maximum_fusion
  194.4 0.0 copy-start.3
  194.4 0.0 copy-start.1
  194.4 0.0 all-to-all-done.3.back
  194.4 8.5 %all-to-all-start.2 = ((bf16[128,2,64,128]{3,2,1,0:T(8,128)(2,1)}), bf16[128,2,64,128]{3,2,1,0:T(8,128)(2,1)}, u32[]{:S(2)}, u32[]{:S(2)}) async-start(bf16[128,2,64,128]{3,2,1,0:T(8,128)(2,1)} %bitcast.39), calls=%async_computation.2 | async-start | bytes 8388608 | tf_op jit(solution)/shard_map/all_to_all | solution.py:459
  203.0 0.0 copy-done.2
  203.0 0.1 copy.8
  203.1 0.0 copy-done.3
  203.1 0.1 iota_compare_fusion
  203.2 0.1 lt.47
  203.3 0.7 reshape_squeeze.3.block_rows
  204.0 0.1 broadcast_multiply_fusion
  204.1 0.7 broadcast_select_fusion.cells
  204.8 2.0 multiply_multiply_fusion
  206.9 1.2 fusion.19
  208.1 1.2 fusion.16
  209.3 1.2 fusion.13
  210.5 1.2 fusion.10
  211.8 1.2 fusion.7
  213.0 1.2 fusion.4
  214.2 7.8 %misfit.1.early = bf16[60,64,128]{2,1,0:T(8,128)(2,1)} custom-call(s32[256]{0:T(256)} %bitcast.53, s32[1,256]{1,0:T(1,128)} %reshape_squeeze.3.block_rows, s32[256,128]{1,0:T(8,128)} %broadcast_select_fusion.cells, bf16[128,2,64,128]{3,2,1,0:T(8,128)(2,1)} %all-to-all-done.3.back, bf16[60,128,128]{2,1,0:T(8,128)(2,1)} %get-tuple-element.15.filt), custom_call_target="tpu_custom_call" | custom-call | bytes 8126464 | tf_op jit(solution)/shard_map/misfit/pallas_call | solution.py:339
  222.0 30.0 %all-to-all-done.2.back = bf16[128,2,64,128]{3,2,1,0:T(8,128)(2,1)} async-done(((bf16[128,2,64,128]{3,2,1,0:T(8,128)(2,1)}), bf16[128,2,64,128]{3,2,1,0:T(8,128)(2,1)}, u32[]{:S(2)}, u32[]{:S(2)}) %all-to-all-start.2) | async-done | bytes 4194336 | tf_op jit(solution)/shard_map/all_to_all | solution.py:459
  252.0 9.3 %adjoint.1 = f32[7680,128]{1,0:T(8,128)} custom-call(s32[256]{0:T(256)} %bitcast.54, s32[1,256]{1,0:T(1,128)} %reshape_squeeze.3.block_rows, s32[256,128]{1,0:T(8,128)} %broadcast_select_fusion.cells, bf16[128,2,64,128]{3,2,1,0:T(8,128)(2,1)} %all-to-all-done.2.back, bf16[60,128,128]{2,1,0:T(8,128)(2,1)} %get-tuple-element.15.filt, ...), custom_call_target="tpu_custom_call" | custom-call | bytes 8126464 | tf_op jit(solution)/shard_map/adjoint/pallas_call | solution.py:339
  (4 shorter events, 0.0 us)
Async XLA Ops:
  7.9 62.4 %all-to-all-start = ((bf16[128,136,128]{2,1,0:T(8,128)(2,1)}), bf16[128,136,128]{2,1,0:T(8,128)(2,1)}, u32[]{:S(2)}, u32[]{:S(2)}) async-start(bf16[128,136,128]{2,1,0:T(8,128)(2,1)} %get-tuple-element.14), calls=%async_computation | async-start | bytes 8912896 | tf_op jit(solution)/shard_map/all_to_all | solution.py:432
  70.3 57.4 %all-to-all-start.1 = ((bf16[128,2,64,128]{3,2,1,0:T(8,128)(2,1)}), bf16[128,2,64,128]{3,2,1,0:T(8,128)(2,1)}, u32[]{:S(2)}, u32[]{:S(2)}) async-start(bf16[128,2,64,128]{3,2,1,0:T(8,128)(2,1)} %late.1), calls=%async_computation.1 | async-start | bytes 8388608 | tf_op jit(solution)/shard_map/all_to_all | solution.py:434
  127.7 66.7 %all-to-all-start.3 = ((bf16[128,2,64,128]{3,2,1,0:T(8,128)(2,1)}), bf16[128,2,64,128]{3,2,1,0:T(8,128)(2,1)}, u32[]{:S(2)}, u32[]{:S(2)}) async-start(bf16[128,2,64,128]{3,2,1,0:T(8,128)(2,1)} %bitcast.40), calls=%async_computation.3 | async-start | bytes 8388608 | tf_op jit(solution)/shard_map/all_to_all | solution.py:441
  152.6 29.3 %collective-permute-start = (f32[2,48,128]{2,1,0:T(8,128)S(1)}, f32[2,48,128]{2,1,0:T(8,128)S(1)}, u32[]{:S(2)}, u32[]{:S(2)}) collective-permute-start(f32[2,48,128]{2,1,0:T(8,128)S(1)} %bitcast.50), channel_id=1, source_target_pairs={{0,16},{16,32},{32,48},{48,64},{64,80},{80,96},{96,112},{1,17},{17... | collective-permute-start | bytes 147464 | tf_op jit(solution)/shard_map/ppermute | solution.py:366
  154.7 27.2 %collective-permute-start.1 = (f32[2,48,128]{2,1,0:T(8,128)S(1)}, f32[2,48,128]{2,1,0:T(8,128)S(1)}, u32[]{:S(2)}, u32[]{:S(2)}) collective-permute-start(f32[2,48,128]{2,1,0:T(8,128)S(1)} %bitcast.49), channel_id=1, source_target_pairs={{16,0},{32,16},{48,32},{64,48},{80,64},{96,80},{112,96},{17,1},{33... | collective-permute-start | bytes 147464 | tf_op jit(solution)/shard_map/ppermute | solution.py:369
  158.2 23.7 %copy-start = (f32[1536,128]{1,0:T(8,128)S(1)}, f32[1536,128]{1,0:T(8,128)}, u32[]{:S(2)}) copy-start(f32[1536,128]{1,0:T(8,128)} %get-tuple-element.18) | copy-start | bytes 2359300
  181.9 6.3 %collective-permute-start.2 = (f32[36,2,128]{2,1,0:T(2,128)S(1)}, f32[36,2,128]{2,1,0:T(2,128)S(1)}, u32[]{:S(2)}, u32[]{:S(2)}) collective-permute-start(f32[36,2,128]{2,1,0:T(2,128)S(1)} %get-tuple-element.32), channel_id=1, source_target_pairs={{0,1},{1,2},{2,3},{3,4},{4,5},{5,6},{6,7},{7,8},{8,9},{9,10},{10,1... | collective-permute-start | bytes 110600 | tf_op jit(solution)/shard_map/ppermute | solution.py:366
  186.3 16.6 %copy-start.2 = (s32[1,128,2]{1,2,0:T(2,128)S(1)}, s32[1,128,2]{1,2,0:T(2,128)}, u32[]{:S(2)}) copy-start(s32[1,128,2]{1,2,0:T(2,128)} %param.7) | copy-start | bytes 3076
  186.3 8.0 %collective-permute-start.3 = (f32[36,2,128]{2,1,0:T(2,128)S(1)}, f32[36,2,128]{2,1,0:T(2,128)S(1)}, u32[]{:S(2)}, u32[]{:S(2)}) collective-permute-start(f32[36,2,128]{2,1,0:T(2,128)S(1)} %get-tuple-element.33), channel_id=1, source_target_pairs={{1,0},{2,1},{3,2},{4,3},{5,4},{6,5},{7,6},{8,7},{9,8},{10,9},{11,1... | collective-permute-start | bytes 110600 | tf_op jit(solution)/shard_map/ppermute | solution.py:369
  194.4 8.7 %copy-start.3 = (s32[1,128]{1,0:T(1,128)S(1)}, s32[1,128]{1,0:T(1,128)}, u32[]{:S(2)}) copy-start(s32[1,128]{1,0:T(1,128)} %param.9) | copy-start | bytes 1540
  194.4 9.7 %copy-start.1 = (s32[1,128,2,128]{3,2,1,0:T(2,128)S(1)}, s32[1,128,2,128]{3,2,1,0:T(2,128)}, u32[]{:S(2)}) copy-start(s32[1,128,2,128]{3,2,1,0:T(2,128)} %param.8) | copy-start | bytes 393220
  194.4 57.6 %all-to-all-start.2 = ((bf16[128,2,64,128]{3,2,1,0:T(8,128)(2,1)}), bf16[128,2,64,128]{3,2,1,0:T(8,128)(2,1)}, u32[]{:S(2)}, u32[]{:S(2)}) async-start(bf16[128,2,64,128]{3,2,1,0:T(8,128)(2,1)} %bitcast.39), calls=%async_computation.2 | async-start | bytes 8388608 | tf_op jit(solution)/shard_map/all_to_all | solution.py:459
